TPU v7x, 1024 devices: a whole 4x4x32 slice. The times are simulated.
1024 devices in a mesh: space: 64 (over z, core), vel: 16 (over y, x).
Axes of the slice: x: 4, y: 4, z: 32, core: 2. Of those that a mesh axis runs over, the one named last changes fastest.
Arguments:
- dist: float32 [64, 512, 4096], P('space', None, 'vel'), may hold values from 0.1 to 10
- neighbours: int32 [64, 6], P('space'), may hold values from -1 to 63, as said below
- solid: int32 [64, 512], P('space'), may hold values 0 or 1
Outputs:
- final_dist: float32 [64, 512, 4096], P('space', None, 'vel')
Inputs may be any that keep to these rules, and one draw needn't show every extreme that they name: `neighbours`: each entry is -1 or a block held by the same index of space as block b (blocks b * 1 onwards) or by the index just below or just above it, cyclically over the space axis.
All inputs are finite; a program needn't handle non-finite values. No bound on the sum of `solid` on one device may be relied on, other than what follows from the above.
Results may differ from a plain program's by a relative error of at most 0.0003.
Values sent between devices are 32-bit elements; how exact they have to be, the bound alone decides.
No kernel may reach another device: no remote copies, remote signals or barrier semaphores. Data moves between devices by JAX's collectives and lax.ppermute only.
A program may use at most 32 MiB of HBM per device.

v0:
```python
import math

import jax
import jax.numpy as jnp
from jax import lax
from jax.sharding import PartitionSpec as P

NVX = 16
BS = 8
ITERS = 2


velocity_step = 0.5
diffusivity_ratio = 2.0 / 3.0
viscosity_exponent = 0.19
rarefaction_ratio = 100.0
courant = 0.9


def with_halo(block, sides, width):
    for axis, dim in sides:
        count = lax.axis_size(axis)
        forward = [(i, i + 1) for i in range(count - 1)]
        forward.append((count - 1, 0))
        backward = [(target, source) for source, target in forward]
        low = lax.ppermute(
            lax.slice_in_dim(block, block.shape[dim] - width, None, axis=dim), axis, forward
        )
        high = lax.ppermute(lax.slice_in_dim(block, 0, width, axis=dim), axis, backward)
        block = jnp.concatenate([low, block, high], axis=dim)
    return block


def timestep_length():
    return courant / (1.5 * (NVX - 1) * velocity_step)


def velocity_grid(first_index, local_count):
    indices = first_index + jnp.arange(local_count, dtype=jnp.int32)
    along_x = indices // (NVX * NVX)
    along_y = indices // NVX % NVX
    along_z = indices % NVX
    centre = (NVX - 1) / 2.0
    return tuple(
        (
            (axis_index.astype(jnp.float32) - centre) * velocity_step
            for axis_index in (along_x, along_y, along_z)
        )
    )


def gaussian_population(
    molecule_concentration,
    bulk_flow_first,
    bulk_flow_second,
    bulk_flow_third,
    kinetic_heat_level,
    molecule_motion_grid,
):
    random_motion_width = (
        (molecule_motion_grid[0] - bulk_flow_first) ** 2
        + (molecule_motion_grid[1] - bulk_flow_second) ** 2
        + (molecule_motion_grid[2] - bulk_flow_third) ** 2
    )
    return (
        molecule_concentration
        * (2.0 * math.pi * kinetic_heat_level) ** (-1.5)
        * jnp.exp(-random_motion_width / (2.0 * kinetic_heat_level))
    )


def boundary_layers(volume):
    leading = volume.shape[0]
    trailing = volume.shape[-1]
    pieces = [
        volume[:, 0],
        volume[:, -1],
        volume[:, :, 0],
        volume[:, :, -1],
        volume[:, :, :, 0],
        volume[:, :, :, -1],
    ]
    return jnp.stack([piece.reshape(leading, BS * BS, trailing) for piece in pieces], axis=1)


def transport(volume, ghosts, molecule_motion_grid):
    leading = volume.shape[0]
    trailing = volume.shape[-1]
    shaped = ghosts.reshape(leading, 6, BS, BS, trailing)
    behind_x = jnp.concatenate([shaped[:, 0][:, None], volume[:, :-1]], axis=1)
    ahead_x = jnp.concatenate([volume[:, 1:], shaped[:, 1][:, None]], axis=1)
    behind_y = jnp.concatenate([shaped[:, 2][:, :, None], volume[:, :, :-1]], axis=2)
    ahead_y = jnp.concatenate([volume[:, :, 1:], shaped[:, 3][:, :, None]], axis=2)
    behind_z = jnp.concatenate([shaped[:, 4][:, :, :, None], volume[:, :, :, :-1]], axis=3)
    ahead_z = jnp.concatenate([volume[:, :, :, 1:], shaped[:, 5][:, :, :, None]], axis=3)
    upwind = jnp.maximum(molecule_motion_grid[0], 0.0) * (volume - behind_x) + jnp.minimum(
        molecule_motion_grid[0], 0.0
    ) * (ahead_x - volume)
    upwind = (
        upwind
        + jnp.maximum(molecule_motion_grid[1], 0.0) * (volume - behind_y)
        + jnp.minimum(molecule_motion_grid[1], 0.0) * (ahead_y - volume)
    )
    upwind = (
        upwind
        + jnp.maximum(molecule_motion_grid[2], 0.0) * (volume - behind_z)
        + jnp.minimum(molecule_motion_grid[2], 0.0) * (ahead_z - volume)
    )
    return volume - timestep_length() * upwind


def primary_integrals(grid_site_values, molecule_motion_grid):
    weight = velocity_step**3
    unity = jnp.ones_like(molecule_motion_grid[0])
    second_power = (
        molecule_motion_grid[0] ** 2 + molecule_motion_grid[1] ** 2 + molecule_motion_grid[2] ** 2
    )
    weights_table = (
        jnp.stack(
            [
                unity,
                molecule_motion_grid[0],
                molecule_motion_grid[1],
                molecule_motion_grid[2],
                second_power,
            ]
        )
        * weight
    )
    return lax.dot_general(
        weights_table,
        grid_site_values,
        (((1,), (1,)), ((), ())),
        precision=lax.Precision.HIGHEST,
        preferred_element_type=jnp.float32,
    )


def hydrodynamic_quantities(primary_totals):
    molecule_concentration = primary_totals[0]
    bulk_flow_vector = primary_totals[1:4] / molecule_concentration
    kinetic_heat_level = (
        primary_totals[4] / molecule_concentration
        - jnp.sum(bulk_flow_vector * bulk_flow_vector, axis=0)
    ) / 3.0
    return (molecule_concentration, bulk_flow_vector, kinetic_heat_level)


def heat_terms(grid_site_values, molecule_motion_grid, bulk_flow_vector):
    weight = velocity_step**3
    relative = [
        molecule_motion_grid[axis_number][None, :] - bulk_flow_vector[axis_number][:, None]
        for axis_number in range(3)
    ]
    second_power = relative[0] ** 2 + relative[1] ** 2 + relative[2] ** 2
    return (
        jnp.stack([jnp.sum(part * second_power * grid_site_values, axis=1) for part in relative])
        * weight
    )


def collision_correction(
    grid_site_values,
    molecule_concentration,
    bulk_flow_vector,
    kinetic_heat_level,
    interface_transfers,
    molecule_motion_grid,
):
    relative = [
        molecule_motion_grid[axis_number][None, :] - bulk_flow_vector[axis_number][:, None]
        for axis_number in range(3)
    ]
    second_power = relative[0] ** 2 + relative[1] ** 2 + relative[2] ** 2
    mass_per_volume_vector = molecule_concentration[:, None]
    heat_level_vector = kinetic_heat_level[:, None]
    target_population = (
        mass_per_volume_vector
        * (2.0 * math.pi * heat_level_vector) ** (-1.5)
        * jnp.exp(-second_power / (2.0 * heat_level_vector))
    )
    normal_stress = mass_per_volume_vector * heat_level_vector
    subspace_mapping = (
        relative[0] * interface_transfers[0][:, None]
        + relative[1] * interface_transfers[1][:, None]
        + relative[2] * interface_transfers[2][:, None]
    )
    heat_corrected_model = target_population * (
        1.0
        + (1.0 - diffusivity_ratio)
        * subspace_mapping
        / (5.0 * normal_stress * heat_level_vector)
        * (second_power / heat_level_vector - 5.0)
    )
    collision_frequency = (
        timestep_length()
        * mass_per_volume_vector
        * heat_level_vector**viscosity_exponent
        / rarefaction_ratio
    )
    return (grid_site_values + collision_frequency * heat_corrected_model) / (
        1.0 + collision_frequency
    )


def on_device(dist, neighbours, solid):
    blocks, block_cells, local_vel = dist.shape
    molecule_motion_grid = velocity_grid(lax.axis_index("vel") * local_vel, local_vel)
    wall_state = gaussian_population(20.0, 0.0, 0.0, 0.0, 2.0, molecule_motion_grid)
    inflow = gaussian_population(20.0, 2.5, 0.0, 0.0, 1.0, molecule_motion_grid)
    opposite = jnp.array([1, 0, 3, 2, 5, 4], dtype=jnp.int32)
    all_blocks = blocks * lax.axis_size("space")
    lowest = (lax.axis_index("space") - 1) * blocks
    opened = neighbours < 0
    nearby = jnp.where(opened, 0, jnp.mod(neighbours - lowest, all_blocks))
    solid_cells = solid[:, :, None] == 1
    flat_cells = blocks * block_cells
    present_dist = dist
    for repeat in range(ITERS):
        filled = jnp.where(solid_cells, wall_state, present_dist)
        volume = filled.reshape(blocks, BS, BS, BS, local_vel)
        layers = boundary_layers(volume)
        extended = with_halo(layers, (("space", 0),), blocks)
        chosen = nearby * 6 + opposite[None, :]
        ghosts = extended.reshape(3 * blocks * 6, BS * BS, local_vel)[chosen]
        ghosts = jnp.where(opened[:, :, None, None], inflow, ghosts)
        advected_population = transport(volume, ghosts, molecule_motion_grid).reshape(
            flat_cells, local_vel
        )
        primary_totals = lax.psum(
            primary_integrals(advected_population, molecule_motion_grid), "vel"
        )
        molecule_concentration, bulk_flow_vector, kinetic_heat_level = hydrodynamic_quantities(
            primary_totals
        )
        interface_transfers = lax.psum(
            heat_terms(advected_population, molecule_motion_grid, bulk_flow_vector), "vel"
        )
        present_dist = collision_correction(
            advected_population,
            molecule_concentration,
            bulk_flow_vector,
            kinetic_heat_level,
            interface_transfers,
            molecule_motion_grid,
        ).reshape(blocks, block_cells, local_vel)
    return jnp.where(solid_cells, wall_state, present_dist)


def solution(mesh):
    in_specs = (P("space", None, "vel"), P("space", None), P("space", None))
    out_specs = P("space", None, "vel")
    return jax.shard_map(
        on_device, mesh=mesh, in_specs=in_specs, out_specs=out_specs, check_vma=False
    )
```

profile of v0, /device:TPU:2, one launch (start us, length us, event | category | flops | bytes accessed | tf_op | source)
XLA Modules:
  0.0 272.3 jit_solution(2897792717213897864)
XLA Ops:
  0.0 0.7 compare_reduce_fusion
  0.7 1.2 broadcast_select_fusion
  2.1 16.2 %collective-permute-start.1 = (f32[1,6,64,256]{3,2,1,0:T(8,128)S(1)}, f32[1,6,64,256]{3,2,1,0:T(8,128)S(1)}, u32[]{:S(2)}, u32[]{:S(2)}) collective-permute-start(f32[1,6,64,256]{3,2,1,0:T(8,128)S(1)} %fusion.116), channel_id=1, source_target_pairs={{16,0},{32,16},{48,32},{64,48},{80,64},{96,80},{112,96},{128,112},... | collective-permute-start | bytes 1179656 | tf_op jit(solution)/shard_map/ppermute | solution.py:29
  19.1 1.0 fusion.149
  21.3 0.6 broadcast_maximum_fusion.1
  23.9 0.8 copy-done.10
  24.7 2.2 collective-permute-done
  26.9 1.2 pad_maximum_fusion
  28.1 0.7 gather_fusion
  28.8 0.8 bitcast_select_fusion.1
  30.2 0.8 copy-done.6
  32.6 69.6 %psum.28 = f32[5,512]{1,0:T(8,128)S(1)} all-reduce(f32[5,512]{1,0:T(8,128)S(1)} %fusion.120), channel_id=1, replica_groups=mesh['space'=64,'vel'=16] {'vel'}, use_global_device_ids=true, to_apply=%region_0.1 | all-reduce | flops 2560 | bytes 20480 | tf_op jit(solution)/shard_map/psum | solution.py:230
  102.8 41.5 %psum.29 = f32[3,512]{1,0:T(4,128)S(1)} all-reduce(f32[3,512]{1,0:T(4,128)S(1)} %maximum_multiply_fusion), channel_id=1, replica_groups=mesh['space'=64,'vel'=16] {'vel'}, use_global_device_ids=true, to_apply=%region_5.6 | all-reduce | flops 1536 | bytes 12288 | tf_op jit(solution)/shard_map/psum | solution.py:236
  144.4 2.4 fusion.18
  147.5 1.0 fusion.146
  148.5 0.9 fusion.145
  149.5 2.8 %collective-permute-done.3 = f32[1,6,64,256]{3,2,1,0:T(8,128)S(1)} collective-permute-done((f32[1,6,64,256]{3,2,1,0:T(8,128)S(1)}, f32[1,6,64,256]{3,2,1,0:T(8,128)S(1)}, u32[]{:S(2)}, u32[]{:S(2)}) %collective-permute-start.3) | collective-permute-done | bytes 393248 | tf_op jit(solution)/shard_map/ppermute | solution.py:29
  152.3 3.1 %collective-permute-done.2 = f32[1,6,64,256]{3,2,1,0:T(8,128)S(1)} collective-permute-done((f32[1,6,64,256]{3,2,1,0:T(8,128)S(1)}, f32[1,6,64,256]{3,2,1,0:T(8,128)S(1)}, u32[]{:S(2)}, u32[]{:S(2)}) %collective-permute-start.2) | collective-permute-done | bytes 393248 | tf_op jit(solution)/shard_map/ppermute | solution.py:26
  155.5 1.5 gather_fusion.1
  157.0 1.1 bitcast_select_fusion
  158.5 0.7 copy-done.9
  161.2 66.1 %psum.30 = f32[5,512]{1,0:T(8,128)S(1)} all-reduce(f32[5,512]{1,0:T(8,128)S(1)} %fusion.118), channel_id=1, replica_groups=mesh['space'=64,'vel'=16] {'vel'}, use_global_device_ids=true, to_apply=%region_6.7 | all-reduce | flops 2560 | bytes 20480 | tf_op jit(solution)/shard_map/psum | solution.py:230
  228.0 41.3 %psum.31 = f32[3,512]{1,0:T(4,128)S(1)} all-reduce(f32[3,512]{1,0:T(4,128)S(1)} %maximum_multiply_fusion.1), channel_id=1, replica_groups=mesh['space'=64,'vel'=16] {'vel'}, use_global_device_ids=true, to_apply=%region_11.12 | all-reduce | flops 1536 | bytes 12288 | tf_op jit(solution)/shard_map/psum | solution.py:236
  269.3 3.0 %fusion.44 = f32[1,512,256]{2,1,0:T(8,128)} fusion(f32[1,512,256]{2,1,0:T(8,128)S(1)} %fusion.18, f32[1,8,8,8,256]{4,3,2,1,0:T(8,128)S(1)} %pad_maximum_fusion.13, f32[1,8,8,8,256]{4,3,2,1,0:T(8,128)S(1)} %pad_maximum_fusion.12, f32[1,8,8,8,256]{4,3,2,1,0:T(8,128)S(1)} %pad_maximum_fusion.11, f32[1,8,8,8,256]{4,3,2,1,0:T(8,128)S(1)} %pad_maximum_fusion.10, ...), kind=kLoop, calls=%fused_computation.72 | loop fusion | flops 6029312 | bytes 4229632 | tf_op jit(solution)/shard_map/jit(_where)/select_n | solution.py:247
  (121 shorter events, 10.5 us)
Async XLA Ops:
  0.0 1.9 copy-start.12
  0.7 1.2 copy-start.20
  2.1 21.8 %collective-permute-start.1 = (f32[1,6,64,256]{3,2,1,0:T(8,128)S(1)}, f32[1,6,64,256]{3,2,1,0:T(8,128)S(1)}, u32[]{:S(2)}, u32[]{:S(2)}) collective-permute-start(f32[1,6,64,256]{3,2,1,0:T(8,128)S(1)} %fusion.116), channel_id=1, source_target_pairs={{16,0},{32,16},{48,32},{64,48},{80,64},{96,80},{112,96},{128,112},... | collective-permute-start | bytes 1179656 | tf_op jit(solution)/shard_map/ppermute | solution.py:29
  18.3 8.5 %collective-permute-start = (f32[1,6,64,256]{3,2,1,0:T(8,128)S(1)}, f32[1,6,64,256]{3,2,1,0:T(8,128)}, u32[]{:S(2)}, u32[]{:S(2)}) collective-permute-start(f32[1,6,64,256]{3,2,1,0:T(8,128)S(1)} %fusion.116), channel_id=1, source_target_pairs={{0,16},{16,32},{32,48},{48,64},{64,80},{80,96},{96,112},{112,128},... | collective-permute-start | bytes 1179656 | tf_op jit(solution)/shard_map/ppermute | solution.py:26
  19.0 2.9 %copy-start.24 = (s32[1,6]{1,0:T(1,128)S(1)}, s32[1,6]{1,0:T(1,128)}, u32[]{:S(2)}) copy-start(s32[1,6]{1,0:T(1,128)} %param.5) | copy-start | bytes 76
  19.0 3.5 %copy-start.25 = (s32[1,6]{1,0:T(1,128)S(1)}, s32[1,6]{1,0:T(1,128)}, u32[]{:S(2)}) copy-start(s32[1,6]{1,0:T(1,128)} %constant.150) | copy-start | bytes 76
  30.0 1.0 copy-start.6
  30.1 1.1 copy-start.5
  30.1 1.2 copy-start.2
  30.1 1.2 copy-start.13
  30.1 1.2 copy-start.14
  30.2 1.2 copy-start.15
  30.2 1.2 copy-start.16
  30.2 1.2 copy-start.17
  30.2 1.2 copy-start.18
  30.2 1.2 copy-start.19
  30.2 1.2 copy-start.21
  31.4 70.8 %copy-start.11 = (f32[256]{0:T(256)S(1)}, f32[256]{0:T(256)}, u32[]{:S(2)}) copy-start(f32[256]{0:T(256)} %get-tuple-element.81) | copy-start | bytes 3076
  146.9 5.3 %collective-permute-start.3 = (f32[1,6,64,256]{3,2,1,0:T(8,128)S(1)}, f32[1,6,64,256]{3,2,1,0:T(8,128)S(1)}, u32[]{:S(2)}, u32[]{:S(2)}) collective-permute-start(f32[1,6,64,256]{3,2,1,0:T(8,128)S(1)} %fusion.114), channel_id=1, source_target_pairs={{16,0},{32,16},{48,32},{64,48},{80,64},{96,80},{112,96},{128,112},... | collective-permute-start | bytes 1179656 | tf_op jit(solution)/shard_map/ppermute | solution.py:29
  147.0 8.4 %collective-permute-start.2 = (f32[1,6,64,256]{3,2,1,0:T(8,128)S(1)}, f32[1,6,64,256]{3,2,1,0:T(8,128)S(1)}, u32[]{:S(2)}, u32[]{:S(2)}) collective-permute-start(f32[1,6,64,256]{3,2,1,0:T(8,128)S(1)} %fusion.114), channel_id=1, source_target_pairs={{0,16},{16,32},{32,48},{48,64},{64,80},{80,96},{96,112},{112,128},... | collective-permute-start | bytes 1179656 | tf_op jit(solution)/shard_map/ppermute | solution.py:26
  149.4 7.5 %copy-start.22 = (f32[256]{0:T(256)S(1)}, f32[256]{0:T(256)}, u32[]{:S(2)}) copy-start(f32[256]{0:T(256)} %get-tuple-element.74) | copy-start | bytes 3076
  149.4 7.5 %copy-start.23 = (pred[6]{0:T(512)(128)(4,1)S(1)}, pred[6]{0:T(512)(128)(4,1)}, u32[]{:S(2)}) copy-start(pred[6]{0:T(512)(128)(4,1)} %compare_bitcast_fusion) | copy-start | bytes 22
  158.4 1.1 copy-start.8
  158.5 1.1 copy-start.7
  (6 other events, 5.2 us)
where the time goes:
time: 273 us; the launch traced here: 272 us
  blocking collectives  219 us (80%)
  other arithmetic  17.7 us (6%)
  starting transfers between devices  16.7 us (6%)
  local copies, waits for them, and re-layouts  9.49 us (3%)
  waiting for transfers between devices  8.15 us (3%)
    psum x2, blocking collectives, on_device(): lax.psum(primary_integrals(advected_population, molecule_motion_grid), 'v...  136 us
    psum x2, blocking collectives, on_device(): lax.psum(heat_terms(advected_population, molecule_motion_grid, bulk_flow_...  82.8 us
    ppermute x2, starting transfers between devices, with_halo(): lax.ppermute(lax.slice_in_dim(block, 0, width, axis=dim), axis, backward)  16.2 us
  transfers between devices with their start and end apart: 4, of which 3 were waited for; matrix products, arithmetic and copies ran while one was open for 3% of the time, Pallas kernels for 0%

commit v1 on v0

v1 whole, which is shorter than its diff:
```python
import math

import jax
import jax.numpy as jnp
from jax import lax
from jax.experimental import pallas as pl
from jax.experimental.pallas import tpu as pltpu
from jax.sharding import PartitionSpec as P

NVX = 16
BS = 8
ITERS = 2
CELLS = BS * BS * BS
GROUPS = BS * BS
LANES = NVX * NVX
HALF = LANES // 2

velocity_step = 0.5
diffusivity_ratio = 2.0 / 3.0
viscosity_exponent = 0.19
rarefaction_ratio = 100.0
courant = 0.9
dt = courant / (1.5 * (NVX - 1) * velocity_step)
weight = velocity_step**3
centre = (NVX - 1) / 2.0

F32 = jnp.float32


def lane_velocities(rows=1):
    lane = lax.broadcasted_iota(jnp.int32, (rows, LANES), 1)
    cy = ((lane >> 4).astype(F32) - centre) * velocity_step
    cz = ((lane & (NVX - 1)).astype(F32) - centre) * velocity_step
    return cy, cz


def own_cx():
    return (lax.axis_index("vel").astype(F32) - centre) * velocity_step


def maxwellian(rho, ux, temperature, cx, cy, cz):
    width = (cx - ux) * (cx - ux) + cy * cy + cz * cz
    return rho * (2.0 * math.pi * temperature) ** (-1.5) * jnp.exp(width * (-0.5 / temperature))


def store_faces(filled, faces):
    _, cz = lane_velocities(GROUPS)
    positive = lax.axis_index("vel") >= NVX // 2
    first = pl.multiple_of(jnp.where(positive, (BS - 1) * GROUPS, 0), GROUPS)
    for half in range(2):
        faces[half, 0] = filled[half, pl.ds(first, GROUPS), :]
        for i in range(BS):
            row = i * GROUPS + half * (BS - 1) * BS
            faces[half, 1, i * BS : (i + 1) * BS, :] = filled[half, row : row + BS, :]
        bottom = filled[half, pl.ds(0, GROUPS, stride=BS), :]
        top = filled[half, pl.ds(BS - 1, GROUPS, stride=BS), :]
        upward = cz[:, half * HALF : (half + 1) * HALF] > 0
        faces[half, 2] = jnp.where(upward, top, bottom)


def fill_kernel(dist, solid, filled, faces):
    cx = own_cx()
    cy, cz = lane_velocities()
    wall = maxwellian(20.0, 0.0, 2.0, cx, cy, cz)
    flags = jnp.broadcast_to(solid[...].astype(F32), (BS, CELLS))
    top = lax.broadcasted_iota(jnp.int32, (BS, HALF), 0) == 0
    mask = lax.dot_general(
        flags, top.astype(F32), (((0,), (0,)), ((), ())), preferred_element_type=F32
    )
    inside = mask > 0.5
    for half in range(2):
        lanes = slice(half * HALF, (half + 1) * HALF)
        filled[half] = jnp.where(inside, wall[:, lanes], dist[:, lanes])
    store_faces(filled, faces)


def advect_kernel(neighbours, filled, own, below, above, advected, partial, ghost_z):
    cx = own_cx()
    cy, cz = lane_velocities()
    here = lax.axis_index("space")
    count = lax.axis_size("space")
    inflow = maxwellian(20.0, 2.5, 1.0, cx, cy, cz)

    def pick(face, dim, half):
        block = neighbours[0, face]
        place = lax.rem(block - here + 1 + count, count)
        value = jnp.where(place == 0, below[half, dim], above[half, dim])
        value = jnp.where(place == 1, own[half, dim], value)
        return jnp.where(block < 0, inflow[:, half * HALF : (half + 1) * HALF], value)

    positive = lax.axis_index("vel") >= NVX // 2
    face_x = jnp.where(positive, 0, 1)
    kx = dt * jnp.abs(cx)
    ky = dt * jnp.abs(cy)
    kz = dt * jnp.abs(cz)
    keep = 1.0 - kx - ky - kz
    sub = lax.broadcasted_iota(jnp.int32, (BS, HALF), 0)
    row_weights = []
    for half in range(2):
        lanes = slice(half * HALF, (half + 1) * HALF)
        upward = jnp.broadcast_to(cz[:, lanes] > 0, (BS, HALF))
        edge = (sub == 0) & upward | (sub == BS - 1) & jnp.logical_not(upward)
        gx = pick(face_x, 0, half)
        gy = pick(3 if half == 0 else 2, 1, half)
        up64 = jnp.broadcast_to(cz[:, lanes] > 0, (GROUPS, HALF))
        ghost_z[half] = jnp.where(up64, pick(4, 2, half), pick(5, 2, half))
        k0 = jnp.broadcast_to(keep[:, lanes], (BS, HALF))
        k2 = jnp.broadcast_to(ky[:, lanes], (BS, HALF))
        k3 = jnp.broadcast_to(kz[:, lanes], (BS, HALF))
        for i in range(BS):
            for j in range(BS):
                row = (i * BS + j) * BS
                value = filled[half, row : row + BS]
                down_row = max(row - GROUPS, 0)
                up_row = min(row + GROUPS, CELLS - BS)
                x_low = filled[half, down_row : down_row + BS]
                x_high = filled[half, up_row : up_row + BS]
                if i == 0:
                    x_low = gx[j * BS : (j + 1) * BS]
                if i == BS - 1:
                    x_high = gx[j * BS : (j + 1) * BS]
                x_up = jnp.where(positive, x_low, x_high)
                if half == 0:
                    y_up = (
                        filled[half, row + BS : row + 2 * BS]
                        if j < BS - 1
                        else gy[i * BS : (i + 1) * BS]
                    )
                else:
                    y_up = (
                        filled[half, row - BS : row] if j > 0 else gy[i * BS : (i + 1) * BS]
                    )
                group = i * BS + j
                z_up = jnp.where(upward, pltpu.roll(value, 1, 0), pltpu.roll(value, BS - 1, 0))
                z_ghost = jnp.broadcast_to(ghost_z[half, group : group + 1], (BS, HALF))
                z_up = jnp.where(edge, z_ghost, z_up)
                advected[half, row : row + BS] = k0 * value + kx * x_up + k2 * y_up + k3 * z_up
    one = jnp.ones_like(cy)
    plane = cy * cy + cz * cz
    table = jnp.concatenate(
        [one, cy, cz, cy * cy, cz * cz, cy * cz, cy * plane, cz * plane], axis=0
    )
    total = None
    for half in range(2):
        term = lax.dot_general(
            table[:, half * HALF : (half + 1) * HALF] * weight,
            advected[half],
            (((1,), (1,)), ((), ())),
            precision=lax.Precision.HIGHEST,
            preferred_element_type=F32,
        )
        total = term if total is None else total + term
    partial[...] = total


def collide_kernel(gathered, solid, advected, out, faces, turned):
    sums = [jnp.zeros((BS, CELLS), F32) for _ in range(4)]
    for a in range(NVX):
        ca = (a - centre) * velocity_step
        part = gathered[a]
        for n in range(4):
            sums[n] = sums[n] + part * ca**n

    def row(n, r):
        return sums[n][r : r + 1, :]

    rho = row(0, 0)
    jx, jy, jz = row(1, 0), row(0, 1), row(0, 2)
    pxx, pyy, pzz = row(2, 0), row(0, 3), row(0, 4)
    pxy, pxz, pyz = row(1, 1), row(1, 2), row(0, 5)
    hx = row(3, 0) + row(1, 3) + row(1, 4)
    hy = row(2, 1) + row(0, 6)
    hz = row(2, 2) + row(0, 7)
    energy = pxx + pyy + pzz
    ux, uy, uz = jx / rho, jy / rho, jz / rho
    speed = ux * ux + uy * uy + uz * uz
    temperature = (energy / rho - speed) / 3.0
    twice = 2.0 * rho * speed
    qx = hx - 2.0 * (ux * pxx + uy * pxy + uz * pxz) - ux * energy + ux * twice
    qy = hy - 2.0 * (ux * pxy + uy * pyy + uz * pyz) - uy * energy + uy * twice
    qz = hz - 2.0 * (ux * pxz + uy * pyz + uz * pzz) - uz * energy + uz * twice
    log_t = jnp.log(temperature)
    rate = (dt / rarefaction_ratio) * rho * jnp.exp(viscosity_exponent * log_t)
    keep = 1.0 / (1.0 + rate)
    amount = rate * keep * rho * (2.0 * math.pi) ** (-1.5) * jnp.exp(-1.5 * log_t)
    scale = ((1.0 - diffusivity_ratio) / 5.0) / (rho * temperature * temperature)
    cx = own_cx()
    rx = cx - ux
    inside = solid[...] == 1
    zero = jnp.zeros_like(rho)
    wall_amount = 20.0 * (2.0 * math.pi * 2.0) ** (-1.5)
    rows = [
        jnp.where(inside, zero, uy),
        jnp.where(inside, zero, uz),
        jnp.where(inside, cx * cx, rx * rx),
        jnp.where(inside, zero, qy * scale),
        jnp.where(inside, zero, qz * scale),
        jnp.where(inside, zero, rx * qx * scale),
        jnp.where(inside, -0.25, -0.5 / temperature),
        jnp.where(inside, wall_amount, amount),
        jnp.where(inside, zero, keep),
    ]
    rows = rows + [zero] * (NVX - len(rows))
    turned[...] = jnp.concatenate(rows, axis=0).T
    cy, cz = lane_velocities(BS)
    for group in range(GROUPS):
        at = slice(group * BS, (group + 1) * BS)
        cell = turned[at, :]

        def wide(k):
            return jnp.broadcast_to(cell[:, k : k + 1], (BS, HALF))

        vy, vz, rx2, sy, sz, sx, slope, top, stay = [wide(k) for k in range(9)]
        for half in range(2):
            lanes = slice(half * HALF, (half + 1) * HALF)
            ry = cy[:, lanes] - vy
            rz = cz[:, lanes] - vz
            exponent = (ry * ry + rz * rz + rx2) * slope
            flow = ry * sy + rz * sz + sx
            shape = 1.0 + flow * (-2.0 * exponent - 5.0)
            value = stay * advected[half, at] + top * jnp.exp(exponent) * shape
            if faces is None:
                out[at, lanes] = value
            else:
                out[half, at] = value
    if faces is not None:
        store_faces(out, faces)


def last_kernel(gathered, solid, advected, out, turned):
    collide_kernel(gathered, solid, advected, out, None, turned)


VMEM = pl.BlockSpec(memory_space=pltpu.VMEM)
SMEM = pl.BlockSpec(memory_space=pltpu.SMEM)
FIELD = jax.ShapeDtypeStruct((2, CELLS, HALF), F32)
RESULT = jax.ShapeDtypeStruct((CELLS, LANES), F32)
FACES = jax.ShapeDtypeStruct((2, 3, GROUPS, HALF), F32)
PARTIAL = jax.ShapeDtypeStruct((BS, CELLS), F32)


def call(kernel, ins, outs, scratch=()):
    return pl.pallas_call(
        kernel,
        in_specs=ins,
        out_specs=[VMEM] * len(outs),
        out_shape=outs,
        scratch_shapes=list(scratch),
        compiler_params=pltpu.CompilerParams(vmem_limit_bytes=16 * 1024 * 1024),
    )


def on_device(dist, neighbours, solid):
    count = lax.axis_size("space")
    forward = [(i, (i + 1) % count) for i in range(count)]
    backward = [(target, source) for source, target in forward]
    filled, faces = call(fill_kernel, [VMEM] * 2, [FIELD, FACES])(dist[0], solid)
    for step in range(ITERS):
        below = lax.ppermute(faces, "space", forward)
        above = lax.ppermute(faces, "space", backward)
        advected, partial = call(
            advect_kernel,
            [SMEM] + [VMEM] * 4,
            [FIELD, PARTIAL],
            [pltpu.VMEM((2, GROUPS, HALF), F32)],
        )(neighbours, filled, faces, below, above)
        copies = jnp.broadcast_to(partial, (NVX, BS, CELLS))
        gathered = lax.all_to_all(copies, "vel", 0, 0, tiled=True)
        turned = [pltpu.VMEM((CELLS, NVX), F32)]
        if step < ITERS - 1:
            filled, faces = call(collide_kernel, [VMEM] * 3, [FIELD, FACES], turned)(
                gathered, solid, advected
            )
        else:
            (filled,) = call(last_kernel, [VMEM] * 3, [RESULT], turned)(gathered, solid, advected)
    return filled[None]


def solution(mesh):
    in_specs = (P("space", None, "vel"), P("space", None), P("space", None))
    out_specs = P("space", None, "vel")
    return jax.shard_map(
        on_device, mesh=mesh, in_specs=in_specs, out_specs=out_specs, check_vma=False
    )
```

time: 273 us -> 63.5 us (0.23)
  blocking collectives: 219 us -> 26.2 us
  other arithmetic: 17.7 us -> 0 us
  local copies, waits for them, and re-layouts: 9.49 us -> 1.84 us
  Pallas kernels: 0 us -> 6.3 us
  waiting for transfers between devices: 8.15 us -> 12.1 us
    psum x4 -> x0, blocking collectives: 219 us -> none  [the longest x2 136 us: on_device(): lax.psum(primary_integrals(advected_population, molecule_motion_grid), 'v...]
    all_to_all x0 -> x2, blocking collectives: none -> 26.2 us  [on_device(): gathered = lax.all_to_all(copies, 'vel', 0, 0, tiled=True)]
    select_n x5 -> x0, other arithmetic: 8.46 us -> none  [the longest x2 3.56 us: on_device(): filled = jnp.where(solid_cells, wall_state, present_dist)]
    pallas_call x0 -> x5, Pallas kernels: none -> 6.3 us  [the longest x2 2.52 us: on_device(): call(advect_kernel, [SMEM] + [VMEM] * 4, [FIELD, PARTIAL], [pltpu.VMEM((2...]
    ppermute x4, waiting for transfers between devices: 8.15 us -> 12.1 us  [the longest x2 6.25 us: on_device(): below = lax.ppermute(faces, 'space', forward)]
    slice x16 -> x0, local copies, waits for them, and re-layouts: 3.37 us -> none  [the longest x4 1.94 us: transport(): behind_x = jnp.concatenate([shaped[:, 0][:, None], volume[:, :-1]], axis=1)]
  transfers between devices with their start and end apart: 4 -> 4, of which waited for: 3 -> 4; matrix products, arithmetic and copies ran while one was open for 3% -> 0% of each run, Pallas kernels for 0% -> 0%
where the time goes in v1:
time: 63.5 us; the launch traced here: 63.3 us
  blocking collectives  26.2 us (41%)
  starting transfers between devices  16.7 us (26%)
  waiting for transfers between devices  12.1 us (19%)
  Pallas kernels  6.3 us (10%)
  local copies, waits for them, and re-layouts  1.84 us (3%)
    all_to_all x2, blocking collectives, on_device(): gathered = lax.all_to_all(copies, 'vel', 0, 0, tiled=True)  26.2 us
    ppermute x2, starting transfers between devices, on_device(): above = lax.ppermute(faces, 'space', backward)  16.2 us
    ppermute x2, waiting for transfers between devices, on_device(): below = lax.ppermute(faces, 'space', forward)  6.25 us
    ppermute x2, waiting for transfers between devices, on_device(): above = lax.ppermute(faces, 'space', backward)  5.87 us
    pallas_call x2, Pallas kernels, on_device(): call(advect_kernel, [SMEM] + [VMEM] * 4, [FIELD, PARTIAL], [pltpu.VMEM((2...  2.52 us
    pallas_call x1, Pallas kernels, on_device(): call(last_kernel, [VMEM] * 3, [RESULT], turned)(gathered, solid, advected)  2.13 us
    unnamed x8, local copies, waits for them, and re-layouts  1.73 us
    pallas_call x1, Pallas kernels, on_device(): call(collide_kernel, [VMEM] * 3, [FIELD, FACES], turned)  1.35 us
  transfers between devices with their start and end apart: 4, of which 4 were waited for; matrix products, arithmetic and copies ran while one was open for 0% of the time, Pallas kernels for 0%

profile of v1, /device:TPU:2, one launch (start us, length us, event | category | flops | bytes accessed | tf_op | source)
XLA Modules:
  0.0 63.3 jit_solution(12996021832495014779)
XLA Ops:
  0.0 0.0 copy-start
  0.0 1.0 %copy-done = f32[1,512,256]{2,1,0:T(8,128)S(1)} copy-done((f32[1,512,256]{2,1,0:T(8,128)S(1)}, f32[1,512,256]{2,1,0:T(8,128)}, u32[]{:S(2)}) %copy-start) | copy-done | bytes 524312
  1.0 0.7 %copy-done.1 = s32[1,512]{1,0:T(1,128)S(1)} copy-done((s32[1,512]{1,0:T(1,128)S(1)}, s32[1,512]{1,0:T(1,128)}, u32[]{:S(2)}) %copy-start.1) | copy-done | bytes 2072
  1.7 0.3 shard_map.37
  2.0 0.0 copy-start.3
  2.0 16.2 %collective-permute-start.1 = (f32[2,3,64,128]{3,2,1,0:T(8,128)S(1)}, f32[2,3,64,128]{3,2,1,0:T(8,128)S(1)}, u32[]{:S(2)}, u32[]{:S(2)}) collective-permute-start(f32[2,3,64,128]{3,2,1,0:T(8,128)S(1)} %get-tuple-element.14.own), channel_id=1, source_target_pairs={{16,0},{32,16},{48,32},{64,48},{80,64},{96,80},{112,96},{128,112},... | collective-permute-start | bytes 589832 | tf_op jit(solution)/shard_map/ppermute | solution.py:260
  18.3 0.0 collective-permute-start
  18.3 3.2 %collective-permute-done.1.above = f32[2,3,64,128]{3,2,1,0:T(8,128)S(1)} collective-permute-done((f32[2,3,64,128]{3,2,1,0:T(8,128)S(1)}, f32[2,3,64,128]{3,2,1,0:T(8,128)S(1)}, u32[]{:S(2)}, u32[]{:S(2)}) %collective-permute-start.1) | collective-permute-done | bytes 196640 | tf_op jit(solution)/shard_map/ppermute | solution.py:260
  21.4 3.1 %collective-permute-done.below = f32[2,3,64,128]{3,2,1,0:T(8,128)S(1)} collective-permute-done((f32[2,3,64,128]{3,2,1,0:T(8,128)S(1)}, f32[2,3,64,128]{3,2,1,0:T(8,128)S(1)}, u32[]{:S(2)}, u32[]{:S(2)}) %collective-permute-start) | collective-permute-done | bytes 196640 | tf_op jit(solution)/shard_map/ppermute | solution.py:259
  24.6 0.0 copy-done.3
  24.6 1.3 %shard_map.38 = (f32[2,512,128]{2,1,0:T(8,128)S(1)}, f32[8,512]{1,0:T(8,128)S(1)}) custom-call(s32[1,6]{1,0:T(1,128)S(1)} %copy-done.3, f32[2,512,128]{2,1,0:T(8,128)S(1)} %get-tuple-element.13.filled, f32[2,3,64,128]{3,2,1,0:T(8,128)S(1)} %get-tuple-element.14.own, f32[2,3,64,128]{3,2,1,0:T(8,128)S(1)} %collective-permute-done.below, ...), custom_call_target="tpu_custom_call" | custom-call | tf_op jit(solution)/shard_map/pallas_call | solution.py:261
  25.8 0.1 broadcast_in_dim.9
  25.9 0.0 copy-start.2
  25.9 14.6 %all_to_all.10.gathered = f32[16,8,512]{2,1,0:T(8,128)S(1)} all-to-all(f32[16,8,512]{2,1,0:T(8,128)S(1)} %broadcast_in_dim.9), channel_id=1, replica_groups=mesh['space'=64,'vel'=16] {'vel'}, dimensions={0} | all-to-all | bytes 524288 | tf_op jit(solution)/shard_map/all_to_all | solution.py:268
  40.5 0.0 copy-done.2
  40.5 1.4 %shard_map.39 = (f32[2,512,128]{2,1,0:T(8,128)S(1)}, f32[2,3,64,128]{3,2,1,0:T(8,128)S(1)}) custom-call(f32[16,8,512]{2,1,0:T(8,128)S(1)} %all_to_all.10.gathered, s32[1,512]{1,0:T(1,128)S(1)} %copy-done.2, f32[2,512,128]{2,1,0:T(8,128)S(1)} %get-tuple-element.16.advected), custom_call_target="tpu_custom_call" | custom-call | tf_op jit(solution)/shard_map/pallas_call | solution.py:271
  41.9 0.0 collective-permute-start.3
  41.9 0.5 collective-permute-start.2
  42.4 2.7 %collective-permute-done.3.above = f32[2,3,64,128]{3,2,1,0:T(8,128)S(1)} collective-permute-done((f32[2,3,64,128]{3,2,1,0:T(8,128)S(1)}, f32[2,3,64,128]{3,2,1,0:T(8,128)S(1)}, u32[]{:S(2)}, u32[]{:S(2)}) %collective-permute-start.3) | collective-permute-done | bytes 196640 | tf_op jit(solution)/shard_map/ppermute | solution.py:260
  45.1 3.1 %collective-permute-done.2.below = f32[2,3,64,128]{3,2,1,0:T(8,128)S(1)} collective-permute-done((f32[2,3,64,128]{3,2,1,0:T(8,128)S(1)}, f32[2,3,64,128]{3,2,1,0:T(8,128)S(1)}, u32[]{:S(2)}, u32[]{:S(2)}) %collective-permute-start.2) | collective-permute-done | bytes 196640 | tf_op jit(solution)/shard_map/ppermute | solution.py:259
  48.2 1.3 %shard_map.40 = (f32[2,512,128]{2,1,0:T(8,128)S(1)}, f32[8,512]{1,0:T(8,128)S(1)}) custom-call(s32[1,6]{1,0:T(1,128)S(1)} %copy-done.3, f32[2,512,128]{2,1,0:T(8,128)S(1)} %get-tuple-element.17.filled, f32[2,3,64,128]{3,2,1,0:T(8,128)S(1)} %get-tuple-element.18.own, f32[2,3,64,128]{3,2,1,0:T(8,128)S(1)} %collective-permute-done.2.below, ...), custom_call_target="tpu_custom_call" | custom-call | tf_op jit(solution)/shard_map/pallas_call | solution.py:261
  49.5 0.1 broadcast_in_dim.10
  49.5 11.6 %all_to_all.11.gathered = f32[16,8,512]{2,1,0:T(8,128)S(1)} all-to-all(f32[16,8,512]{2,1,0:T(8,128)S(1)} %broadcast_in_dim.10), channel_id=1, replica_groups=mesh['space'=64,'vel'=16] {'vel'}, dimensions={0} | all-to-all | bytes 524288 | tf_op jit(solution)/shard_map/all_to_all | solution.py:268
  61.1 2.1 %shard_map.41 = f32[512,256]{1,0:T(8,128)} custom-call(f32[16,8,512]{2,1,0:T(8,128)S(1)} %all_to_all.11.gathered, s32[1,512]{1,0:T(1,128)S(1)} %copy-done.2, f32[2,512,128]{2,1,0:T(8,128)S(1)} %get-tuple-element.20.advected), custom_call_target="tpu_custom_call" | custom-call | tf_op jit(solution)/shard_map/pallas_call | solution.py:275
  (1 shorter events, 0.0 us)
Async XLA Ops:
  0.0 1.0 %copy-start = (f32[1,512,256]{2,1,0:T(8,128)S(1)}, f32[1,512,256]{2,1,0:T(8,128)}, u32[]{:S(2)}) copy-start(f32[1,512,256]{2,1,0:T(8,128)} %param.3) | copy-start | bytes 1572868
  1.0 0.7 %copy-start.1 = (s32[1,512]{1,0:T(1,128)S(1)}, s32[1,512]{1,0:T(1,128)}, u32[]{:S(2)}) copy-start(s32[1,512]{1,0:T(1,128)} %solid.5) | copy-start | bytes 6148
  2.0 22.5 %copy-start.3 = (s32[1,6]{1,0:T(1,128)S(1)}, s32[1,6]{1,0:T(1,128)}, u32[]{:S(2)}) copy-start(s32[1,6]{1,0:T(1,128)} %neighbours.3) | copy-start | bytes 76
  2.0 19.4 %collective-permute-start.1 = (f32[2,3,64,128]{3,2,1,0:T(8,128)S(1)}, f32[2,3,64,128]{3,2,1,0:T(8,128)S(1)}, u32[]{:S(2)}, u32[]{:S(2)}) collective-permute-start(f32[2,3,64,128]{3,2,1,0:T(8,128)S(1)} %get-tuple-element.14.own), channel_id=1, source_target_pairs={{16,0},{32,16},{48,32},{64,48},{80,64},{96,80},{112,96},{128,112},... | collective-permute-start | bytes 589832 | tf_op jit(solution)/shard_map/ppermute | solution.py:260
  18.3 6.3 %collective-permute-start = (f32[2,3,64,128]{3,2,1,0:T(8,128)S(1)}, f32[2,3,64,128]{3,2,1,0:T(8,128)S(1)}, u32[]{:S(2)}, u32[]{:S(2)}) collective-permute-start(f32[2,3,64,128]{3,2,1,0:T(8,128)S(1)} %get-tuple-element.14.own), channel_id=1, source_target_pairs={{0,16},{16,32},{32,48},{48,64},{64,80},{80,96},{96,112},{112,128},... | collective-permute-start | bytes 589832 | tf_op jit(solution)/shard_map/ppermute | solution.py:259
  25.9 14.6 %copy-start.2 = (s32[1,512]{1,0:T(1,128)S(1)}, s32[1,512]{1,0:T(1,128)}, u32[]{:S(2)}) copy-start(s32[1,512]{1,0:T(1,128)} %solid.5) | copy-start | bytes 6148
  41.9 3.2 %collective-permute-start.3 = (f32[2,3,64,128]{3,2,1,0:T(8,128)S(1)}, f32[2,3,64,128]{3,2,1,0:T(8,128)S(1)}, u32[]{:S(2)}, u32[]{:S(2)}) collective-permute-start(f32[2,3,64,128]{3,2,1,0:T(8,128)S(1)} %get-tuple-element.18.own), channel_id=1, source_target_pairs={{16,0},{32,16},{48,32},{64,48},{80,64},{96,80},{112,96},{128,112},... | collective-permute-start | bytes 589832 | tf_op jit(solution)/shard_map/ppermute | solution.py:260
  41.9 6.3 %collective-permute-start.2 = (f32[2,3,64,128]{3,2,1,0:T(8,128)S(1)}, f32[2,3,64,128]{3,2,1,0:T(8,128)S(1)}, u32[]{:S(2)}, u32[]{:S(2)}) collective-permute-start(f32[2,3,64,128]{3,2,1,0:T(8,128)S(1)} %get-tuple-element.18.own), channel_id=1, source_target_pairs={{0,16},{16,32},{32,48},{48,64},{64,80},{80,96},{96,112},{112,128},... | collective-permute-start | bytes 589832 | tf_op jit(solution)/shard_map/ppermute | solution.py:259

commit v2 on v1

v2 whole, which is shorter than its diff:
```python
import math

import jax
import jax.numpy as jnp
from jax import lax
from jax.experimental import pallas as pl
from jax.experimental.pallas import tpu as pltpu
from jax.sharding import PartitionSpec as P


NVX = 16
BS = 8
ITERS = 2
CELLS = BS * BS * BS
GROUPS = BS * BS
LANES = NVX * NVX
HALF = LANES // 2

velocity_step = 0.5
diffusivity_ratio = 2.0 / 3.0
viscosity_exponent = 0.19
rarefaction_ratio = 100.0
courant = 0.9
dt = courant / (1.5 * (NVX - 1) * velocity_step)
weight = velocity_step**3
centre = (NVX - 1) / 2.0

F32 = jnp.float32


def lane_velocities(rows=1):
    lane = lax.broadcasted_iota(jnp.int32, (rows, LANES), 1)
    cy = ((lane >> 4).astype(F32) - centre) * velocity_step
    cz = ((lane & (NVX - 1)).astype(F32) - centre) * velocity_step
    return cy, cz


def own_cx():
    return (lax.axis_index("vel").astype(F32) - centre) * velocity_step


def maxwellian(rho, ux, temperature, cx, cy, cz):
    width = (cx - ux) * (cx - ux) + cy * cy + cz * cz
    return rho * (2.0 * math.pi * temperature) ** (-1.5) * jnp.exp(width * (-0.5 / temperature))


def store_faces(filled, faces):
    _, cz = lane_velocities(GROUPS)
    positive = lax.axis_index("vel") >= NVX // 2
    first = pl.multiple_of(jnp.where(positive, (BS - 1) * GROUPS, 0), GROUPS)
    for half in range(2):
        faces[half, 0] = filled[half, pl.ds(first, GROUPS), :]
        for i in range(BS):
            row = i * GROUPS + half * (BS - 1) * BS
            faces[half, 1, i * BS : (i + 1) * BS, :] = filled[half, row : row + BS, :]
        bottom = filled[half, pl.ds(0, GROUPS, stride=BS), :]
        top = filled[half, pl.ds(BS - 1, GROUPS, stride=BS), :]
        upward = cz[:, half * HALF : (half + 1) * HALF] > 0
        faces[half, 2] = jnp.where(upward, top, bottom)


def fill_kernel(dist_hbm, solid_hbm, filled, faces, dist, solid, sems):
    copies = [
        pltpu.make_async_copy(solid_hbm, solid, sems.at[0]),
        pltpu.make_async_copy(dist_hbm, dist, sems.at[1]),
    ]
    for copy in copies:
        copy.start()
    cx = own_cx()
    cy, cz = lane_velocities()
    wall = maxwellian(20.0, 0.0, 2.0, cx, cy, cz)
    top = lax.broadcasted_iota(jnp.int32, (BS, HALF), 0) == 0
    copies[0].wait()
    flags = jnp.broadcast_to(solid[...].astype(F32), (BS, CELLS))
    mask = lax.dot_general(
        flags, top.astype(F32), (((0,), (0,)), ((), ())), preferred_element_type=F32
    )
    inside = mask > 0.5
    copies[1].wait()
    for half in range(2):
        lanes = slice(half * HALF, (half + 1) * HALF)
        filled[half] = jnp.where(inside, wall[:, lanes], dist[:, lanes])
    store_faces(filled, faces)


def upwind_edge(cz, sub):
    upward = jnp.broadcast_to(cz > 0, (BS, HALF))
    return upward, (sub == 0) & upward | (sub == BS - 1) & jnp.logical_not(upward)


def inner_kernel(filled, inner):
    cx = own_cx()
    cy, cz = lane_velocities()
    positive = lax.axis_index("vel") >= NVX // 2
    kx = dt * jnp.abs(cx)
    ky = dt * jnp.abs(cy)
    kz = dt * jnp.abs(cz)
    keep = 1.0 - kx - ky - kz
    sub = lax.broadcasted_iota(jnp.int32, (BS, HALF), 0)
    for half in range(2):
        lanes = slice(half * HALF, (half + 1) * HALF)
        upward, edge = upwind_edge(cz[:, lanes], sub)
        k0 = jnp.broadcast_to(keep[:, lanes], (BS, HALF))
        k2 = jnp.broadcast_to(ky[:, lanes], (BS, HALF))
        k3 = jnp.where(edge, 0.0, jnp.broadcast_to(kz[:, lanes], (BS, HALF)))
        low_x = jnp.where(positive, kx, 0.0)
        high_x = jnp.where(positive, 0.0, kx)
        for i in range(BS):
            for j in range(BS):
                row = (i * BS + j) * BS
                value = filled[half, row : row + BS]
                total = k0 * value
                if i > 0:
                    total = total + low_x * filled[half, row - GROUPS : row - GROUPS + BS]
                if i < BS - 1:
                    total = total + high_x * filled[half, row + GROUPS : row + GROUPS + BS]
                if half == 0 and j < BS - 1:
                    total = total + k2 * filled[half, row + BS : row + 2 * BS]
                if half == 1 and j > 0:
                    total = total + k2 * filled[half, row - BS : row]
                z_up = jnp.where(upward, pltpu.roll(value, 1, 0), pltpu.roll(value, BS - 1, 0))
                inner[half, row : row + BS] = total + k3 * z_up


def ghost_kernel(neighbours, inner, own, below, above, advected, partial, ghost_z):
    cx = own_cx()
    cy, cz = lane_velocities()
    here = lax.axis_index("space")
    count = lax.axis_size("space")
    inflow = maxwellian(20.0, 2.5, 1.0, cx, cy, cz)

    block = neighbours[...]
    places = jnp.where(block < 0, 3, lax.rem(block - here + 1 + count, count))

    def pick(place, dim, half):
        place = jnp.broadcast_to(place, (GROUPS, HALF))
        value = jnp.where(place == 0, below[half, dim], above[half, dim])
        value = jnp.where(place == 1, own[half, dim], value)
        return jnp.where(place == 3, inflow[:, half * HALF : (half + 1) * HALF], value)

    positive = lax.axis_index("vel") >= NVX // 2
    face = [places[:, k : k + 1] for k in range(6)]
    face_x = jnp.where(positive, face[0], face[1])
    first = pl.multiple_of(jnp.where(positive, 0, (BS - 1) * GROUPS), GROUPS)
    kx = dt * jnp.abs(cx)
    ky = dt * jnp.abs(cy)
    kz = dt * jnp.abs(cz)
    sub = lax.broadcasted_iota(jnp.int32, (BS, HALF), 0)
    one = jnp.ones_like(cy)
    plane = cy * cy + cz * cz
    table = weight * jnp.concatenate(
        [one, cy, cz, cy * cy, cz * cz, cy * cz, cy * plane, cz * plane], axis=0
    )
    coarse = table.astype(jnp.bfloat16)
    table = jnp.concatenate([coarse.astype(F32), table - coarse.astype(F32)], axis=0)
    table = table.astype(jnp.bfloat16)
    total = jnp.zeros((2 * BS, CELLS), F32)
    for half in range(2):
        lanes = slice(half * HALF, (half + 1) * HALF)
        _, edge = upwind_edge(cz[:, lanes], sub)
        side = edge.astype(F32)
        up64 = jnp.broadcast_to(cz[:, lanes] > 0, (GROUPS, HALF))
        ghost_z[half] = kz[:, lanes] * jnp.where(up64, pick(face[4], 2, half), pick(face[5], 2, half))
        gy = ky[:, lanes] * pick(face[3 - half], 1, half)
        gx = kx * pick(face_x, 0, half)
        for i in range(BS):
            for j in range(BS):
                group = i * BS + j
                at = slice(group * BS, (group + 1) * BS)
                z_ghost = jnp.broadcast_to(ghost_z[half, group : group + 1], (BS, HALF))
                value = inner[half, at] + side * z_ghost
                if j == (BS - 1 if half == 0 else 0):
                    value = value + gy[i * BS : (i + 1) * BS]
                advected[half, at] = value
        rows = pl.ds(first, GROUPS)
        advected[half, rows] = advected[half, rows] + gx
        value = advected[half]
        high = value.astype(jnp.bfloat16)
        low = (value - high.astype(F32)).astype(jnp.bfloat16)
        for piece in (high, low):
            total = total + lax.dot_general(
                table[:, lanes],
                piece,
                (((1,), (1,)), ((), ())),
                preferred_element_type=F32,
            )
    partial[...] = total[:BS] + total[BS:]


def bfloat_pieces(value):
    pieces = []
    for _ in range(3):
        piece = value.astype(jnp.bfloat16).astype(F32)
        pieces.append(piece)
        value = value - piece
    return pieces


def cell_basis():
    cy, cz = lane_velocities(NVX)
    row = lax.broadcasted_iota(jnp.int32, (NVX, LANES), 0)
    zero = jnp.zeros((NVX, LANES), F32)

    def rows(first, entries):
        out = zero
        for k, entry in enumerate(entries):
            out = jnp.where(row == first + k, entry, out)
        return out

    exponent = rows(0, [cy * cy + cz * cz, cy, cz, 1.0])
    flow = rows(4, [cy, cz, 1.0])
    stay = rows(7, [1.0])[:, :HALF]
    top = rows(8, [1.0])[:, :HALF]
    block = jnp.concatenate([exponent, flow, stay, top], axis=1)
    return jnp.concatenate([block] * 3, axis=0).astype(jnp.bfloat16)


def collide(gathered, solid, advected, turned, store):
    sums = [None] * 4
    for a in range(NVX // 2, NVX):
        ca = (a - centre) * velocity_step
        high, low = gathered[a], gathered[NVX - 1 - a]
        even, odd = high + low, high - low
        terms = [even, ca * odd, ca**2 * even, ca**3 * odd]
        sums = [t if s is None else s + t for s, t in zip(sums, terms)]

    def row(n, r):
        return sums[n][r : r + 1, :]

    rho = row(0, 0)
    jx, jy, jz = row(1, 0), row(0, 1), row(0, 2)
    pxx, pyy, pzz = row(2, 0), row(0, 3), row(0, 4)
    pxy, pxz, pyz = row(1, 1), row(1, 2), row(0, 5)
    hx = row(3, 0) + row(1, 3) + row(1, 4)
    hy = row(2, 1) + row(0, 6)
    hz = row(2, 2) + row(0, 7)
    energy = pxx + pyy + pzz
    inverse = 1.0 / rho
    ux, uy, uz = jx * inverse, jy * inverse, jz * inverse
    speed = ux * ux + uy * uy + uz * uz
    temperature = (energy * inverse - speed) / 3.0
    twice = 2.0 * rho * speed - energy
    qx = hx - 2.0 * (ux * pxx + uy * pxy + uz * pxz) + ux * twice
    qy = hy - 2.0 * (ux * pxy + uy * pyy + uz * pyz) + uy * twice
    qz = hz - 2.0 * (ux * pxz + uy * pyz + uz * pzz) + uz * twice
    log_t = jnp.log(temperature)
    cold = 1.0 / temperature
    rate = (dt / rarefaction_ratio) * rho * jnp.exp(viscosity_exponent * log_t)
    keep = 1.0 / (1.0 + rate)
    amount = rate * keep * rho * (2.0 * math.pi) ** (-1.5) * jnp.exp(-1.5 * log_t)
    scale = ((1.0 - diffusivity_ratio) / 5.0) * inverse * cold * cold
    cx = own_cx()
    rx = cx - ux
    slope = -0.5 * cold
    sy, sz = qy * scale, qz * scale
    inside = solid[...] == 1
    wall_amount = 20.0 * (2.0 * math.pi * 2.0) ** (-1.5)
    rows = [
        jnp.where(inside, -0.25, slope),
        jnp.where(inside, 0.0, cold * uy),
        jnp.where(inside, 0.0, cold * uz),
        jnp.where(inside, -0.25 * (cx * cx), slope * (rx * rx + uy * uy + uz * uz)),
        jnp.where(inside, 0.0, sy),
        jnp.where(inside, 0.0, sz),
        jnp.where(inside, 0.0, rx * qx * scale - sy * uy - sz * uz),
        jnp.where(inside, 0.0, keep),
        jnp.where(inside, wall_amount, amount),
    ]
    rows = rows + [jnp.zeros_like(rho)] * (NVX - len(rows))
    pieces = jnp.concatenate(bfloat_pieces(jnp.concatenate(rows, axis=0)), axis=0)
    turned[...] = pieces.T.astype(jnp.bfloat16)
    basis = cell_basis()
    chunk = 2 * GROUPS
    for first in range(0, CELLS, chunk):
        at = slice(first, first + chunk)
        wide = jnp.dot(turned[at], basis, preferred_element_type=F32)
        stay = wide[:, 2 * LANES : 2 * LANES + HALF]
        top = wide[:, 2 * LANES + HALF :]
        for half in range(2):
            exponent = wide[:, half * HALF : (half + 1) * HALF]
            flow = wide[:, LANES + half * HALF : LANES + (half + 1) * HALF]
            shape = 1.0 + flow * (-2.0 * exponent - 5.0)
            value = stay * advected[half, at] + top * jnp.exp(exponent) * shape
            store(half, first, chunk, value)


def collide_kernel(gathered, solid, advected, filled, faces, turned):
    def store(half, first, count, value):
        filled[half, first : first + count] = value

    collide(gathered, solid, advected, turned, store)
    store_faces(filled, faces)


def last_kernel(gathered, solid, advected, result, turned, out, sems):
    copies = []

    def store(half, first, count, value):
        out[first : first + count, half * HALF : (half + 1) * HALF] = value
        if half == 1:
            at = pl.ds(first, count)
            copy = pltpu.make_async_copy(out.at[at], result.at[at], sems.at[len(copies)])
            copy.start()
            copies.append(copy)

    collide(gathered, solid, advected, turned, store)
    for copy in copies:
        copy.wait()


VMEM = pl.BlockSpec(memory_space=pltpu.VMEM)
HBM = pl.BlockSpec(memory_space=pltpu.HBM)
FIELD = jax.ShapeDtypeStruct((2, CELLS, HALF), F32)
RESULT = jax.ShapeDtypeStruct((CELLS, LANES), F32)
FACES = jax.ShapeDtypeStruct((2, 3, GROUPS, HALF), F32)
PARTIAL = jax.ShapeDtypeStruct((BS, CELLS), F32)
TURNED = pltpu.VMEM((CELLS, 3 * NVX), jnp.bfloat16)


def call(kernel, ins, outs, scratch=(), out_spec=VMEM):
    size = CELLS * LANES
    return pl.pallas_call(
        kernel,
        in_specs=ins,
        out_specs=[out_spec] * len(outs),
        out_shape=outs,
        scratch_shapes=list(scratch),
        cost_estimate=pl.CostEstimate(
            flops=40 * size, transcendentals=size, bytes_accessed=8 * size
        ),
        compiler_params=pltpu.CompilerParams(vmem_limit_bytes=16 * 1024 * 1024),
    )


def on_device(dist, neighbours, solid):
    count = lax.axis_size("space")
    forward = [(i, (i + 1) % count) for i in range(count)]
    backward = [(target, source) for source, target in forward]
    filled, faces = call(
        fill_kernel,
        [HBM] * 2,
        [FIELD, FACES],
        [
            pltpu.VMEM((CELLS, LANES), F32),
            pltpu.VMEM((1, CELLS), jnp.int32),
            pltpu.SemaphoreType.DMA((2,)),
        ],
    )(
        pltpu.with_memory_space_constraint(dist[0], pltpu.HBM),
        pltpu.with_memory_space_constraint(solid, pltpu.HBM),
    )
    for step in range(ITERS):
        below = lax.ppermute(faces, "space", forward)
        above = lax.ppermute(faces, "space", backward)
        (inner,) = call(inner_kernel, [VMEM], [FIELD])(filled)
        advected, partial = call(
            ghost_kernel,
            [VMEM] * 5,
            [FIELD, PARTIAL],
            [pltpu.VMEM((2, GROUPS, HALF), F32)],
        )(neighbours, inner, faces, below, above)
        copies = jnp.broadcast_to(partial, (NVX, BS, CELLS))
        gathered = lax.all_to_all(copies, "vel", 0, 0, tiled=True)
        if step < ITERS - 1:
            filled, faces = call(collide_kernel, [VMEM] * 3, [FIELD, FACES], [TURNED])(
                gathered, solid, advected
            )
        else:
            (filled,) = call(
                last_kernel,
                [VMEM] * 3,
                [RESULT],
                [TURNED, pltpu.VMEM((CELLS, LANES), F32), pltpu.SemaphoreType.DMA((4,))],
                HBM,
            )(gathered, solid, advected)
    return filled[None]


def solution(mesh):
    in_specs = (P("space", None, "vel"), P("space", None), P("space", None))
    out_specs = P("space", None, "vel")
    return jax.shard_map(
        on_device, mesh=mesh, in_specs=in_specs, out_specs=out_specs, check_vma=False
    )
```

time: 63.5 us -> 59.3 us (0.934)
  Pallas kernels: 6.3 us -> 4.29 us
  local copies, waits for them, and re-layouts: 1.84 us -> 0.11 us
    pallas_call x5 -> x7, Pallas kernels: 6.3 us -> 4.29 us  [the longest x1 1.26 us: on_device(): call(last_kernel, [VMEM] * 3, [RESULT], [TURNED, pltpu.VMEM((CELLS, LANES...]
    unnamed x8 -> x4, local copies, waits for them, and re-layouts: 1.73 us -> 0.01 us
  transfers between devices with their start and end apart: 4 -> 4, of which waited for: 4 -> 4; matrix products, arithmetic and copies ran while one was open for 0% -> 0% of each run, Pallas kernels for 0% -> 1%
where the time goes in v2:
time: 59.3 us; the launch traced here: 59.1 us
  blocking collectives  26.2 us (44%)
  starting transfers between devices  16.7 us (28%)
  waiting for transfers between devices  11.7 us (20%)
  Pallas kernels  4.29 us (7%)
    all_to_all x2, blocking collectives, on_device(): gathered = lax.all_to_all(copies, 'vel', 0, 0, tiled=True)  26.2 us
    ppermute x2, starting transfers between devices, on_device(): above = lax.ppermute(faces, 'space', backward)  16.2 us
    ppermute x2, waiting for transfers between devices, on_device(): below = lax.ppermute(faces, 'space', forward)  6.25 us
    ppermute x2, waiting for transfers between devices, on_device(): above = lax.ppermute(faces, 'space', backward)  5.45 us
    pallas_call x1, Pallas kernels, on_device(): call(last_kernel, [VMEM] * 3, [RESULT], [TURNED, pltpu.VMEM((CELLS, LANES...  1.26 us
  transfers between devices with their start and end apart: 4, of which 4 were waited for; matrix products, arithmetic and copies ran while one was open for 0% of the time, Pallas kernels for 1%

profile of v2, /device:TPU:2, one launch (start us, length us, event | category | flops | bytes accessed | tf_op | source)
XLA Modules:
  0.0 59.1 jit_solution(6010969830834241330)
XLA Ops:
  0.0 1.1 %shard_map.37 = (f32[2,512,128]{2,1,0:T(8,128)S(1)}, f32[2,3,64,128]{3,2,1,0:T(8,128)S(1)}) custom-call(f32[512,256]{1,0:T(8,128)} %bitcast.2, s32[1,512]{1,0:T(1,128)} %solid.3), custom_call_target="tpu_custom_call" | custom-call | flops 5242880 | bytes 1048576 | tf_op jit(solution)/shard_map/pallas_call | solution.py:339
  1.2 16.2 %collective-permute-start.1 = (f32[2,3,64,128]{3,2,1,0:T(8,128)S(1)}, f32[2,3,64,128]{3,2,1,0:T(8,128)S(1)}, u32[]{:S(2)}, u32[]{:S(2)}) collective-permute-start(f32[2,3,64,128]{3,2,1,0:T(8,128)S(1)} %get-tuple-element.14.own), channel_id=1, source_target_pairs={{16,0},{32,16},{48,32},{64,48},{80,64},{96,80},{112,96},{128,112},... | collective-permute-start | bytes 589832 | tf_op jit(solution)/shard_map/ppermute | solution.py:354
  17.4 0.0 collective-permute-start
  17.4 0.0 copy-start.1
  17.4 0.2 shard_map.38.inner
  17.6 3.0 %collective-permute-done.1.above = f32[2,3,64,128]{3,2,1,0:T(8,128)S(1)} collective-permute-done((f32[2,3,64,128]{3,2,1,0:T(8,128)S(1)}, f32[2,3,64,128]{3,2,1,0:T(8,128)S(1)}, u32[]{:S(2)}, u32[]{:S(2)}) %collective-permute-start.1) | collective-permute-done | bytes 196640 | tf_op jit(solution)/shard_map/ppermute | solution.py:354
  20.6 3.1 %collective-permute-done.below = f32[2,3,64,128]{3,2,1,0:T(8,128)S(1)} collective-permute-done((f32[2,3,64,128]{3,2,1,0:T(8,128)S(1)}, f32[2,3,64,128]{3,2,1,0:T(8,128)S(1)}, u32[]{:S(2)}, u32[]{:S(2)}) %collective-permute-start) | collective-permute-done | bytes 196640 | tf_op jit(solution)/shard_map/ppermute | solution.py:353
  23.7 0.0 copy-done.1
  23.7 0.4 shard_map.39
  24.2 0.0 copy-start
  24.2 14.6 %all_to_all.10.gathered = f32[16,8,512]{2,1,0:T(8,128)S(1)} all-to-all(f32[16,8,512]{2,1,0:T(8,128)S(1)} %broadcast_in_dim.9), channel_id=1, replica_groups=mesh['space'=64,'vel'=16] {'vel'}, dimensions={0} | all-to-all | bytes 524288 | tf_op jit(solution)/shard_map/all_to_all | solution.py:363
  38.8 0.0 copy-done
  38.8 0.6 %shard_map.40 = (f32[2,512,128]{2,1,0:T(8,128)S(1)}, f32[2,3,64,128]{3,2,1,0:T(8,128)S(1)}) custom-call(f32[16,8,512]{2,1,0:T(8,128)S(1)} %all_to_all.10.gathered, s32[1,512]{1,0:T(1,128)S(1)} %copy-done, f32[2,512,128]{2,1,0:T(8,128)S(1)} %get-tuple-element.16.advected), custom_call_target="tpu_custom_call" | custom-call | flops 5242880 | bytes 1048576 | tf_op jit(solution)/shard_map/pallas_call | solution.py:365
  39.4 0.0 collective-permute-start.3
  39.4 0.5 collective-permute-start.2
  39.9 0.2 shard_map.41.inner
  40.1 2.5 %collective-permute-done.3.above = f32[2,3,64,128]{3,2,1,0:T(8,128)S(1)} collective-permute-done((f32[2,3,64,128]{3,2,1,0:T(8,128)S(1)}, f32[2,3,64,128]{3,2,1,0:T(8,128)S(1)}, u32[]{:S(2)}, u32[]{:S(2)}) %collective-permute-start.3) | collective-permute-done | bytes 196640 | tf_op jit(solution)/shard_map/ppermute | solution.py:354
  42.6 3.1 %collective-permute-done.2.below = f32[2,3,64,128]{3,2,1,0:T(8,128)S(1)} collective-permute-done((f32[2,3,64,128]{3,2,1,0:T(8,128)S(1)}, f32[2,3,64,128]{3,2,1,0:T(8,128)S(1)}, u32[]{:S(2)}, u32[]{:S(2)}) %collective-permute-start.2) | collective-permute-done | bytes 196640 | tf_op jit(solution)/shard_map/ppermute | solution.py:353
  45.7 0.4 shard_map.42
  46.2 11.6 %all_to_all.11.gathered = f32[16,8,512]{2,1,0:T(8,128)S(1)} all-to-all(f32[16,8,512]{2,1,0:T(8,128)S(1)} %broadcast_in_dim.10), channel_id=1, replica_groups=mesh['space'=64,'vel'=16] {'vel'}, dimensions={0} | all-to-all | bytes 524288 | tf_op jit(solution)/shard_map/all_to_all | solution.py:363
  57.8 1.3 %shard_map.43 = f32[512,256]{1,0:T(8,128)} custom-call(f32[16,8,512]{2,1,0:T(8,128)S(1)} %all_to_all.11.gathered, s32[1,512]{1,0:T(1,128)S(1)} %copy-done, f32[2,512,128]{2,1,0:T(8,128)S(1)} %get-tuple-element.20.advected), custom_call_target="tpu_custom_call" | custom-call | flops 5242880 | bytes 1048576 | tf_op jit(solution)/shard_map/pallas_call | solution.py:369
  (2 shorter events, 0.1 us)
Async XLA Ops:
  1.2 19.4 %collective-permute-start.1 = (f32[2,3,64,128]{3,2,1,0:T(8,128)S(1)}, f32[2,3,64,128]{3,2,1,0:T(8,128)S(1)}, u32[]{:S(2)}, u32[]{:S(2)}) collective-permute-start(f32[2,3,64,128]{3,2,1,0:T(8,128)S(1)} %get-tuple-element.14.own), channel_id=1, source_target_pairs={{16,0},{32,16},{48,32},{64,48},{80,64},{96,80},{112,96},{128,112},... | collective-permute-start | bytes 589832 | tf_op jit(solution)/shard_map/ppermute | solution.py:354
  17.4 6.3 %collective-permute-start = (f32[2,3,64,128]{3,2,1,0:T(8,128)S(1)}, f32[2,3,64,128]{3,2,1,0:T(8,128)S(1)}, u32[]{:S(2)}, u32[]{:S(2)}) collective-permute-start(f32[2,3,64,128]{3,2,1,0:T(8,128)S(1)} %get-tuple-element.14.own), channel_id=1, source_target_pairs={{0,16},{16,32},{32,48},{48,64},{64,80},{80,96},{96,112},{112,128},... | collective-permute-start | bytes 589832 | tf_op jit(solution)/shard_map/ppermute | solution.py:353
  17.4 6.3 %copy-start.1 = (s32[1,6]{1,0:T(1,128)S(1)}, s32[1,6]{1,0:T(1,128)}, u32[]{:S(2)}) copy-start(s32[1,6]{1,0:T(1,128)} %neighbours.3) | copy-start | bytes 76
  24.2 14.6 %copy-start = (s32[1,512]{1,0:T(1,128)S(1)}, s32[1,512]{1,0:T(1,128)}, u32[]{:S(2)}) copy-start(s32[1,512]{1,0:T(1,128)} %solid.3) | copy-start | bytes 6148
  39.4 3.2 %collective-permute-start.3 = (f32[2,3,64,128]{3,2,1,0:T(8,128)S(1)}, f32[2,3,64,128]{3,2,1,0:T(8,128)S(1)}, u32[]{:S(2)}, u32[]{:S(2)}) collective-permute-start(f32[2,3,64,128]{3,2,1,0:T(8,128)S(1)} %get-tuple-element.18.own), channel_id=1, source_target_pairs={{16,0},{32,16},{48,32},{64,48},{80,64},{96,80},{112,96},{128,112},... | collective-permute-start | bytes 589832 | tf_op jit(solution)/shard_map/ppermute | solution.py:354
  39.4 6.3 %collective-permute-start.2 = (f32[2,3,64,128]{3,2,1,0:T(8,128)S(1)}, f32[2,3,64,128]{3,2,1,0:T(8,128)S(1)}, u32[]{:S(2)}, u32[]{:S(2)}) collective-permute-start(f32[2,3,64,128]{3,2,1,0:T(8,128)S(1)} %get-tuple-element.18.own), channel_id=1, source_target_pairs={{0,16},{16,32},{32,48},{48,64},{64,80},{80,96},{96,112},{112,128},... | collective-permute-start | bytes 589832 | tf_op jit(solution)/shard_map/ppermute | solution.py:353

commit v3 on v2

--- a/solution.py
+++ b/solution.py
@@ -59,27 +59,33 @@
         faces[half, 2] = jnp.where(upward, top, bottom)
 
 
+PIECES = 4
+PIECE = CELLS // PIECES
+
+
 def fill_kernel(dist_hbm, solid_hbm, filled, faces, dist, solid, sems):
-    copies = [
-        pltpu.make_async_copy(solid_hbm, solid, sems.at[0]),
-        pltpu.make_async_copy(dist_hbm, dist, sems.at[1]),
-    ]
-    for copy in copies:
-        copy.start()
+    flags_copy = pltpu.make_async_copy(solid_hbm, solid, sems.at[PIECES])
+    flags_copy.start()
+    copies = []
+    for piece in range(PIECES):
+        at = pl.ds(piece * PIECE, PIECE)
+        copies.append(pltpu.make_async_copy(dist_hbm.at[at], dist.at[at], sems.at[piece]))
+        copies[-1].start()
     cx = own_cx()
     cy, cz = lane_velocities()
     wall = maxwellian(20.0, 0.0, 2.0, cx, cy, cz)
     top = lax.broadcasted_iota(jnp.int32, (BS, HALF), 0) == 0
-    copies[0].wait()
+    flags_copy.wait()
     flags = jnp.broadcast_to(solid[...].astype(F32), (BS, CELLS))
     mask = lax.dot_general(
         flags, top.astype(F32), (((0,), (0,)), ((), ())), preferred_element_type=F32
     )
-    inside = mask > 0.5
-    copies[1].wait()
-    for half in range(2):
-        lanes = slice(half * HALF, (half + 1) * HALF)
-        filled[half] = jnp.where(inside, wall[:, lanes], dist[:, lanes])
+    for piece, copy in enumerate(copies):
+        copy.wait()
+        at = slice(piece * PIECE, (piece + 1) * PIECE)
+        for half in range(2):
+            lanes = slice(half * HALF, (half + 1) * HALF)
+            filled[half, at] = jnp.where(mask[at] > 0.5, wall[:, lanes], dist[at, lanes])
     store_faces(filled, faces)
 
 
@@ -88,7 +94,28 @@
     return upward, (sub == 0) & upward | (sub == BS - 1) & jnp.logical_not(upward)
 
 
-def inner_kernel(filled, inner):
+def cell_basis():
+    cy, cz = lane_velocities(NVX)
+    row = lax.broadcasted_iota(jnp.int32, (NVX, LANES), 0)
+    zero = jnp.zeros((NVX, LANES), F32)
+
+    def rows(first, entries):
+        out = zero
+        for k, entry in enumerate(entries):
+            out = jnp.where(row == first + k, entry, out)
+        return out
+
+    exponent = rows(0, [cy * cy + cz * cz, cy, cz, 1.0])
+    flow = rows(4, [cy, cz, 1.0])
+    stay = rows(7, [1.0])[:, :HALF]
+    top = rows(8, [1.0])[:, :HALF]
+    block = jnp.concatenate([exponent, flow, stay, top], axis=1)
+    return jnp.concatenate([block] * 3, axis=0).astype(jnp.bfloat16)
+
+
+def inner_kernel(filled, inner, basis=None):
+    if basis is not None:
+        basis[...] = cell_basis()
     cx = own_cx()
     cy, cz = lane_velocities()
     positive = lax.axis_index("vel") >= NVX // 2
@@ -184,7 +211,7 @@
                 (((1,), (1,)), ((), ())),
                 preferred_element_type=F32,
             )
-    partial[...] = total[:BS] + total[BS:]
+    partial[...] = jnp.broadcast_to(total[:BS] + total[BS:], (NVX, BS, CELLS))
 
 
 def bfloat_pieces(value):
@@ -196,26 +223,7 @@
     return pieces
 
 
-def cell_basis():
-    cy, cz = lane_velocities(NVX)
-    row = lax.broadcasted_iota(jnp.int32, (NVX, LANES), 0)
-    zero = jnp.zeros((NVX, LANES), F32)
-
-    def rows(first, entries):
-        out = zero
-        for k, entry in enumerate(entries):
-            out = jnp.where(row == first + k, entry, out)
-        return out
-
-    exponent = rows(0, [cy * cy + cz * cz, cy, cz, 1.0])
-    flow = rows(4, [cy, cz, 1.0])
-    stay = rows(7, [1.0])[:, :HALF]
-    top = rows(8, [1.0])[:, :HALF]
-    block = jnp.concatenate([exponent, flow, stay, top], axis=1)
-    return jnp.concatenate([block] * 3, axis=0).astype(jnp.bfloat16)
-
-
-def collide(gathered, solid, advected, turned, store):
+def collide(gathered, solid, advected, basis, turned, sizes, store):
     sums = [None] * 4
     for a in range(NVX // 2, NVX):
         ca = (a - centre) * velocity_step
@@ -269,11 +277,10 @@
     rows = rows + [jnp.zeros_like(rho)] * (NVX - len(rows))
     pieces = jnp.concatenate(bfloat_pieces(jnp.concatenate(rows, axis=0)), axis=0)
     turned[...] = pieces.T.astype(jnp.bfloat16)
-    basis = cell_basis()
-    chunk = 2 * GROUPS
-    for first in range(0, CELLS, chunk):
+    first = 0
+    for chunk in sizes:
         at = slice(first, first + chunk)
-        wide = jnp.dot(turned[at], basis, preferred_element_type=F32)
+        wide = jnp.dot(turned[at], basis[...], preferred_element_type=F32)
         stay = wide[:, 2 * LANES : 2 * LANES + HALF]
         top = wide[:, 2 * LANES + HALF :]
         for half in range(2):
@@ -282,17 +289,18 @@
             shape = 1.0 + flow * (-2.0 * exponent - 5.0)
             value = stay * advected[half, at] + top * jnp.exp(exponent) * shape
             store(half, first, chunk, value)
-
-
-def collide_kernel(gathered, solid, advected, filled, faces, turned):
+        first += chunk
+
+
+def collide_kernel(gathered, solid, advected, basis, filled, faces, turned):
     def store(half, first, count, value):
         filled[half, first : first + count] = value
 
-    collide(gathered, solid, advected, turned, store)
+    collide(gathered, solid, advected, basis, turned, [PIECE] * PIECES, store)
     store_faces(filled, faces)
 
 
-def last_kernel(gathered, solid, advected, result, turned, out, sems):
+def last_kernel(gathered, solid, advected, basis, result, turned, out, sems):
     copies = []
 
     def store(half, first, count, value):
@@ -303,7 +311,7 @@
             copy.start()
             copies.append(copy)
 
-    collide(gathered, solid, advected, turned, store)
+    collide(gathered, solid, advected, basis, turned, LAST_SIZES, store)
     for copy in copies:
         copy.wait()
 
@@ -313,7 +321,9 @@
 FIELD = jax.ShapeDtypeStruct((2, CELLS, HALF), F32)
 RESULT = jax.ShapeDtypeStruct((CELLS, LANES), F32)
 FACES = jax.ShapeDtypeStruct((2, 3, GROUPS, HALF), F32)
-PARTIAL = jax.ShapeDtypeStruct((BS, CELLS), F32)
+PARTIAL = jax.ShapeDtypeStruct((NVX, BS, CELLS), F32)
+LAST_SIZES = (176, 160, 112, 64)
+BASIS = jax.ShapeDtypeStruct((3 * NVX, 3 * LANES), jnp.bfloat16)
 TURNED = pltpu.VMEM((CELLS, 3 * NVX), jnp.bfloat16)
 
 
@@ -343,7 +353,7 @@
         [
             pltpu.VMEM((CELLS, LANES), F32),
             pltpu.VMEM((1, CELLS), jnp.int32),
-            pltpu.SemaphoreType.DMA((2,)),
+            pltpu.SemaphoreType.DMA((PIECES + 1,)),
         ],
     )(
         pltpu.with_memory_space_constraint(dist[0], pltpu.HBM),
@@ -352,27 +362,29 @@
     for step in range(ITERS):
         below = lax.ppermute(faces, "space", forward)
         above = lax.ppermute(faces, "space", backward)
-        (inner,) = call(inner_kernel, [VMEM], [FIELD])(filled)
+        if step == 0:
+            inner, basis = call(inner_kernel, [VMEM], [FIELD, BASIS])(filled)
+        else:
+            (inner,) = call(inner_kernel, [VMEM], [FIELD])(filled)
         advected, partial = call(
             ghost_kernel,
             [VMEM] * 5,
             [FIELD, PARTIAL],
             [pltpu.VMEM((2, GROUPS, HALF), F32)],
         )(neighbours, inner, faces, below, above)
-        copies = jnp.broadcast_to(partial, (NVX, BS, CELLS))
-        gathered = lax.all_to_all(copies, "vel", 0, 0, tiled=True)
+        gathered = lax.all_to_all(partial, "vel", 0, 0, tiled=True)
         if step < ITERS - 1:
-            filled, faces = call(collide_kernel, [VMEM] * 3, [FIELD, FACES], [TURNED])(
-                gathered, solid, advected
+            filled, faces = call(collide_kernel, [VMEM] * 4, [FIELD, FACES], [TURNED])(
+                gathered, solid, advected, basis
             )
         else:
             (filled,) = call(
                 last_kernel,
-                [VMEM] * 3,
+                [VMEM] * 4,
                 [RESULT],
                 [TURNED, pltpu.VMEM((CELLS, LANES), F32), pltpu.SemaphoreType.DMA((4,))],
                 HBM,
-            )(gathered, solid, advected)
+            )(gathered, solid, advected, basis)
     return filled[None]
 
 

time: 59.3 us -> 60 us (1.012)
    unnamed x4, local copies, waits for them, and re-layouts: 0.01 us -> 0.69 us
    pallas_call x2 -> x3, Pallas kernels: 1.85 us -> 2.06 us  [the longest x1 1.26 us: on_device(): call(last_kernel, [VMEM] * 4, [RESULT], [TURNED, pltpu.VMEM((CELLS, LANES...]
where the time goes in v3:
time: 60 us; the launch traced here: 59.8 us
  blocking collectives  26.2 us (44%)
  starting transfers between devices  16.7 us (28%)
  waiting for transfers between devices  11.7 us (20%)
  Pallas kernels  4.4 us (7%)
  local copies, waits for them, and re-layouts  0.69 us (1%)
    all_to_all x2, blocking collectives, on_device(): gathered = lax.all_to_all(partial, 'vel', 0, 0, tiled=True)  26.2 us
    ppermute x2, starting transfers between devices, on_device(): above = lax.ppermute(faces, 'space', backward)  16.2 us
    ppermute x2, waiting for transfers between devices, on_device(): below = lax.ppermute(faces, 'space', forward)  6.25 us
    ppermute x2, waiting for transfers between devices, on_device(): above = lax.ppermute(faces, 'space', backward)  5.44 us
    pallas_call x1, Pallas kernels, on_device(): call(last_kernel, [VMEM] * 4, [RESULT], [TURNED, pltpu.VMEM((CELLS, LANES...  1.26 us
  transfers between devices with their start and end apart: 4, of which 4 were waited for; matrix products, arithmetic and copies ran while one was open for 0% of the time, Pallas kernels for 1%

profile of v3, /device:TPU:2, one launch (start us, length us, event | category | flops | bytes accessed | tf_op | source)
XLA Modules:
  0.0 59.8 jit_solution(16846535726910715064)
XLA Ops:
  0.0 1.2 %shard_map.37 = (f32[2,512,128]{2,1,0:T(8,128)S(1)}, f32[2,3,64,128]{3,2,1,0:T(8,128)S(1)}) custom-call(f32[512,256]{1,0:T(8,128)} %bitcast.2, s32[1,512]{1,0:T(1,128)} %solid.3), custom_call_target="tpu_custom_call" | custom-call | flops 5242880 | bytes 1048576 | tf_op jit(solution)/shard_map/pallas_call | solution.py:349
  1.2 16.2 %collective-permute-start.1 = (f32[2,3,64,128]{3,2,1,0:T(8,128)S(1)}, f32[2,3,64,128]{3,2,1,0:T(8,128)S(1)}, u32[]{:S(2)}, u32[]{:S(2)}) collective-permute-start(f32[2,3,64,128]{3,2,1,0:T(8,128)S(1)} %get-tuple-element.17.own), channel_id=1, source_target_pairs={{16,0},{32,16},{48,32},{64,48},{80,64},{96,80},{112,96},{128,112},... | collective-permute-start | bytes 589832 | tf_op jit(solution)/shard_map/ppermute | solution.py:364
  17.4 0.0 collective-permute-start
  17.4 0.2 shard_map.38
  17.6 0.0 copy-start.1
  17.6 3.0 %collective-permute-done.1.above = f32[2,3,64,128]{3,2,1,0:T(8,128)S(1)} collective-permute-done((f32[2,3,64,128]{3,2,1,0:T(8,128)S(1)}, f32[2,3,64,128]{3,2,1,0:T(8,128)S(1)}, u32[]{:S(2)}, u32[]{:S(2)}) %collective-permute-start.1) | collective-permute-done | bytes 196640 | tf_op jit(solution)/shard_map/ppermute | solution.py:364
  20.6 3.1 %collective-permute-done.below = f32[2,3,64,128]{3,2,1,0:T(8,128)S(1)} collective-permute-done((f32[2,3,64,128]{3,2,1,0:T(8,128)S(1)}, f32[2,3,64,128]{3,2,1,0:T(8,128)S(1)}, u32[]{:S(2)}, u32[]{:S(2)}) %collective-permute-start) | collective-permute-done | bytes 196640 | tf_op jit(solution)/shard_map/ppermute | solution.py:363
  23.7 0.0 copy-done.1
  23.7 0.5 shard_map.39
  24.2 14.6 %all_to_all.10.gathered = f32[16,8,512]{2,1,0:T(8,128)S(1)} all-to-all(f32[16,8,512]{2,1,0:T(8,128)S(1)} %get-tuple-element.18), channel_id=1, replica_groups=mesh['space'=64,'vel'=16] {'vel'}, dimensions={0} | all-to-all | bytes 524288 | tf_op jit(solution)/shard_map/all_to_all | solution.py:375
  38.8 0.0 copy-start
  38.8 0.7 %copy-done = s32[1,512]{1,0:T(1,128)S(1)} copy-done((s32[1,512]{1,0:T(1,128)S(1)}, s32[1,512]{1,0:T(1,128)}, u32[]{:S(2)}) %copy-start) | copy-done | bytes 2072
  39.5 0.6 shard_map.40
  40.1 0.0 collective-permute-start.3
  40.1 0.5 collective-permute-start.2
  40.6 0.2 shard_map.41.inner
  40.8 2.5 %collective-permute-done.3.above = f32[2,3,64,128]{3,2,1,0:T(8,128)S(1)} collective-permute-done((f32[2,3,64,128]{3,2,1,0:T(8,128)S(1)}, f32[2,3,64,128]{3,2,1,0:T(8,128)S(1)}, u32[]{:S(2)}, u32[]{:S(2)}) %collective-permute-start.3) | collective-permute-done | bytes 196640 | tf_op jit(solution)/shard_map/ppermute | solution.py:364
  43.3 3.1 %collective-permute-done.2.below = f32[2,3,64,128]{3,2,1,0:T(8,128)S(1)} collective-permute-done((f32[2,3,64,128]{3,2,1,0:T(8,128)S(1)}, f32[2,3,64,128]{3,2,1,0:T(8,128)S(1)}, u32[]{:S(2)}, u32[]{:S(2)}) %collective-permute-start.2) | collective-permute-done | bytes 196640 | tf_op jit(solution)/shard_map/ppermute | solution.py:363
  46.4 0.5 shard_map.42
  46.9 11.6 %all_to_all.11.gathered = f32[16,8,512]{2,1,0:T(8,128)S(1)} all-to-all(f32[16,8,512]{2,1,0:T(8,128)S(1)} %get-tuple-element.23), channel_id=1, replica_groups=mesh['space'=64,'vel'=16] {'vel'}, dimensions={0} | all-to-all | bytes 524288 | tf_op jit(solution)/shard_map/all_to_all | solution.py:375
  58.5 1.3 %shard_map.43 = f32[512,256]{1,0:T(8,128)} custom-call(f32[16,8,512]{2,1,0:T(8,128)S(1)} %all_to_all.11.gathered, s32[1,512]{1,0:T(1,128)S(1)} %copy-done, f32[2,512,128]{2,1,0:T(8,128)S(1)} %get-tuple-element.24.advected, bf16[48,768]{1,0:T(8,128)(2,1)S(1)} %get-tuple-element.20.basis), custom_call_target="tpu_custom_call" | custom-call | flops 5242880 | bytes 1048576 | tf_op jit(solution)/shard_map/pallas_call | solution.py:381
Async XLA Ops:
  1.2 19.4 %collective-permute-start.1 = (f32[2,3,64,128]{3,2,1,0:T(8,128)S(1)}, f32[2,3,64,128]{3,2,1,0:T(8,128)S(1)}, u32[]{:S(2)}, u32[]{:S(2)}) collective-permute-start(f32[2,3,64,128]{3,2,1,0:T(8,128)S(1)} %get-tuple-element.17.own), channel_id=1, source_target_pairs={{16,0},{32,16},{48,32},{64,48},{80,64},{96,80},{112,96},{128,112},... | collective-permute-start | bytes 589832 | tf_op jit(solution)/shard_map/ppermute | solution.py:364
  17.4 6.3 %collective-permute-start = (f32[2,3,64,128]{3,2,1,0:T(8,128)S(1)}, f32[2,3,64,128]{3,2,1,0:T(8,128)S(1)}, u32[]{:S(2)}, u32[]{:S(2)}) collective-permute-start(f32[2,3,64,128]{3,2,1,0:T(8,128)S(1)} %get-tuple-element.17.own), channel_id=1, source_target_pairs={{0,16},{16,32},{32,48},{48,64},{64,80},{80,96},{96,112},{112,128},... | collective-permute-start | bytes 589832 | tf_op jit(solution)/shard_map/ppermute | solution.py:363
  17.6 6.1 %copy-start.1 = (s32[1,6]{1,0:T(1,128)S(1)}, s32[1,6]{1,0:T(1,128)}, u32[]{:S(2)}) copy-start(s32[1,6]{1,0:T(1,128)} %neighbours.3) | copy-start | bytes 76
  38.8 0.7 %copy-start = (s32[1,512]{1,0:T(1,128)S(1)}, s32[1,512]{1,0:T(1,128)}, u32[]{:S(2)}) copy-start(s32[1,512]{1,0:T(1,128)} %solid.3) | copy-start | bytes 6148
  40.1 3.2 %collective-permute-start.3 = (f32[2,3,64,128]{3,2,1,0:T(8,128)S(1)}, f32[2,3,64,128]{3,2,1,0:T(8,128)S(1)}, u32[]{:S(2)}, u32[]{:S(2)}) collective-permute-start(f32[2,3,64,128]{3,2,1,0:T(8,128)S(1)} %get-tuple-element.22.own), channel_id=1, source_target_pairs={{16,0},{32,16},{48,32},{64,48},{80,64},{96,80},{112,96},{128,112},... | collective-permute-start | bytes 589832 | tf_op jit(solution)/shard_map/ppermute | solution.py:364
  40.1 6.3 %collective-permute-start.2 = (f32[2,3,64,128]{3,2,1,0:T(8,128)S(1)}, f32[2,3,64,128]{3,2,1,0:T(8,128)S(1)}, u32[]{:S(2)}, u32[]{:S(2)}) collective-permute-start(f32[2,3,64,128]{3,2,1,0:T(8,128)S(1)} %get-tuple-element.22.own), channel_id=1, source_target_pairs={{0,16},{16,32},{32,48},{48,64},{64,80},{80,96},{96,112},{112,128},... | collective-permute-start | bytes 589832 | tf_op jit(solution)/shard_map/ppermute | solution.py:363

commit v4 on v3

--- a/solution.py
+++ b/solution.py
@@ -63,35 +63,109 @@
 PIECE = CELLS // PIECES
 
 
-def fill_kernel(dist_hbm, solid_hbm, filled, faces, dist, solid, sems):
-    flags_copy = pltpu.make_async_copy(solid_hbm, solid, sems.at[PIECES])
-    flags_copy.start()
-    copies = []
-    for piece in range(PIECES):
-        at = pl.ds(piece * PIECE, PIECE)
-        copies.append(pltpu.make_async_copy(dist_hbm.at[at], dist.at[at], sems.at[piece]))
-        copies[-1].start()
+def two_pieces(value):
+    high = value.astype(jnp.bfloat16)
+    return high, (value - high.astype(F32)).astype(jnp.bfloat16)
+
+
+def moment_table():
+    cy, cz = lane_velocities()
+    plane = cy * cy + cz * cz
+    table = weight * jnp.concatenate(
+        [jnp.ones_like(cy), cy, cz, cy * cy, cz * cz, cy * cz, cy * plane, cz * plane], axis=0
+    )
+    return jnp.concatenate([piece.astype(F32) for piece in two_pieces(table)], axis=0)
+
+
+def times_transposed(table, value):
+    total = None
+    for piece in two_pieces(value):
+        term = lax.dot_general(
+            table, piece, (((1,), (1,)), ((), ())), preferred_element_type=F32
+        )
+        total = term if total is None else total + term
+    return total
+
+
+def flux_moments(layer, flux):
+    kx = dt * jnp.abs(own_cx())
+    cy, cz = lane_velocities()
+    ky, kz = dt * jnp.abs(cy), dt * jnp.abs(cz)
+    table = moment_table()
+    rising = jnp.broadcast_to(cz > 0, table.shape)
+    ups, downs = [], []
+    for half in range(2):
+        lanes = slice(half * HALF, (half + 1) * HALF)
+        rows = jnp.concatenate(
+            [layer(half, 0) * kx, layer(half, 1) * ky[:, lanes], layer(half, 2) * kz[:, lanes]],
+            axis=0,
+        )
+        both = jnp.concatenate(
+            [
+                jnp.where(rising[:, lanes], table[:, lanes], 0.0),
+                jnp.where(rising[:, lanes], 0.0, table[:, lanes]),
+            ],
+            axis=0,
+        )
+        term = times_transposed(both.astype(jnp.bfloat16), rows)
+        ups.append(term[0:BS] + term[BS : 2 * BS])
+        downs.append(term[2 * BS : 3 * BS] + term[3 * BS :])
+    sums = [up + down for up, down in zip(ups, downs)]
+    along_x = (sums[0] + sums[1])[:, :GROUPS]
+    flux[0, :, :GROUPS] = along_x
+    flux[0, :, GROUPS:] = jnp.zeros_like(along_x)
+    flux[1, :, :GROUPS] = sums[0][:, GROUPS : 2 * GROUPS]
+    flux[1, :, GROUPS:] = sums[1][:, GROUPS : 2 * GROUPS]
+    flux[2, :, :GROUPS] = (ups[0] + ups[1])[:, 2 * GROUPS :]
+    flux[2, :, GROUPS:] = (downs[0] + downs[1])[:, 2 * GROUPS :]
+
+
+def face_flux(faces, flux):
+    flux_moments(lambda half, dim: faces[half, dim], flux)
+
+
+def fill_kernel(dist_hbm, solid_hbm, filled, faces, flux, solid, dist, sems):
+    copies = [
+        pltpu.make_async_copy(solid_hbm, solid, sems.at[0]),
+        pltpu.make_async_copy(dist_hbm, dist, sems.at[1]),
+    ]
+    for copy in copies:
+        copy.start()
     cx = own_cx()
     cy, cz = lane_velocities()
     wall = maxwellian(20.0, 0.0, 2.0, cx, cy, cz)
     top = lax.broadcasted_iota(jnp.int32, (BS, HALF), 0) == 0
-    flags_copy.wait()
+    copies[0].wait()
     flags = jnp.broadcast_to(solid[...].astype(F32), (BS, CELLS))
     mask = lax.dot_general(
         flags, top.astype(F32), (((0,), (0,)), ((), ())), preferred_element_type=F32
     )
-    for piece, copy in enumerate(copies):
-        copy.wait()
-        at = slice(piece * PIECE, (piece + 1) * PIECE)
-        for half in range(2):
-            lanes = slice(half * HALF, (half + 1) * HALF)
-            filled[half, at] = jnp.where(mask[at] > 0.5, wall[:, lanes], dist[at, lanes])
+    inside = mask > 0.5
+    copies[1].wait()
+    for half in range(2):
+        lanes = slice(half * HALF, (half + 1) * HALF)
+        filled[half] = jnp.where(inside, wall[:, lanes], dist[:, lanes])
     store_faces(filled, faces)
+    face_flux(faces, flux)
 
 
 def upwind_edge(cz, sub):
     upward = jnp.broadcast_to(cz > 0, (BS, HALF))
     return upward, (sub == 0) & upward | (sub == BS - 1) & jnp.logical_not(upward)
+
+
+def spread_table():
+    row = lax.broadcasted_iota(jnp.int32, (2 * GROUPS, CELLS), 0)
+    cell = lax.broadcasted_iota(jnp.int32, (2 * GROUPS, CELLS), 1)
+    place = row & (GROUPS - 1)
+    later = row >= GROUPS
+    positive = lax.axis_index("vel") >= NVX // 2
+    first = jnp.where(positive, 0, (BS - 1) * GROUPS)
+    along_x = jnp.where(later, -1, first + place)
+    along_y = (place >> 3) * GROUPS + (place & (BS - 1)) + jnp.where(later, 0, GROUPS - BS)
+    along_z = place * BS + jnp.where(later, BS - 1, 0)
+    hits = [(cell == target).astype(F32) for target in (along_x, along_y, along_z)]
+    return jnp.concatenate(hits, axis=0).astype(jnp.bfloat16)
 
 
 def cell_basis():
@@ -113,9 +187,17 @@
     return jnp.concatenate([block] * 3, axis=0).astype(jnp.bfloat16)
 
 
-def inner_kernel(filled, inner, basis=None):
-    if basis is not None:
-        basis[...] = cell_basis()
+def first_inner_kernel(filled, inner, local, basis, spread, open_flux):
+    basis[...] = cell_basis()
+    spread[...] = spread_table()
+    cy, cz = lane_velocities()
+    inflow = maxwellian(20.0, 2.5, 1.0, own_cx(), cy, cz)
+    wide = jnp.broadcast_to(inflow, (GROUPS, LANES))
+    flux_moments(lambda half, dim: wide[:, half * HALF : (half + 1) * HALF], open_flux)
+    inner_kernel(filled, inner, local)
+
+
+def inner_kernel(filled, inner, local):
     cx = own_cx()
     cy, cz = lane_velocities()
     positive = lax.axis_index("vel") >= NVX // 2
@@ -147,41 +229,64 @@
                     total = total + k2 * filled[half, row - BS : row]
                 z_up = jnp.where(upward, pltpu.roll(value, 1, 0), pltpu.roll(value, BS - 1, 0))
                 inner[half, row : row + BS] = total + k3 * z_up
-
-
-def ghost_kernel(neighbours, inner, own, below, above, advected, partial, ghost_z):
-    cx = own_cx()
-    cy, cz = lane_velocities()
+    table = moment_table().astype(jnp.bfloat16)
+    total = times_transposed(table[:, :HALF], inner[0])
+    total = total + times_transposed(table[:, HALF:], inner[1])
+    local[...] = total[:BS] + total[BS:]
+
+
+def source_places(neighbours):
+    block = neighbours[...]
     here = lax.axis_index("space")
     count = lax.axis_size("space")
+    places = jnp.where(block < 0, 3, lax.rem(block - here + 1 + count, count))
+    face = [places[:, k : k + 1] for k in range(6)]
+    positive = lax.axis_index("vel") >= NVX // 2
+    return face, jnp.where(positive, face[0], face[1])
+
+
+def choose(place, below, own, above, opened):
+    value = jnp.where(place == 0, below, above)
+    value = jnp.where(place == 1, own, value)
+    return jnp.where(place == 3, opened, value)
+
+
+def join_kernel(neighbours, local, own, below, above, opened, spread, partial):
+    face, face_x = source_places(neighbours)
+    early = lax.broadcasted_iota(jnp.int32, (BS, 2 * GROUPS), 1) < GROUPS
+    places = [
+        jnp.broadcast_to(face_x, early.shape),
+        jnp.where(early, face[3], face[2]),
+        jnp.where(early, face[4], face[5]),
+    ]
+    columns = []
+    for dim, place in enumerate(places):
+        value = choose(place, below[dim], own[dim], above[dim], opened[dim])
+        pieces = bfloat_pieces(value)
+        columns.append(jnp.concatenate(pieces + [jnp.zeros_like(value)], axis=0))
+    left = jnp.concatenate(columns, axis=1).astype(jnp.bfloat16)
+    added = jnp.dot(left, spread[...], preferred_element_type=F32)
+    total = local[...] + (added[:BS] + added[BS : 2 * BS] + added[2 * BS : 3 * BS])
+    partial[...] = jnp.broadcast_to(total, (NVX, BS, CELLS))
+
+
+def ghost_kernel(neighbours, inner, own, below, above, advected, ghost_z):
+    cx = own_cx()
+    cy, cz = lane_velocities()
     inflow = maxwellian(20.0, 2.5, 1.0, cx, cy, cz)
-
-    block = neighbours[...]
-    places = jnp.where(block < 0, 3, lax.rem(block - here + 1 + count, count))
+    face, face_x = source_places(neighbours)
 
     def pick(place, dim, half):
         place = jnp.broadcast_to(place, (GROUPS, HALF))
-        value = jnp.where(place == 0, below[half, dim], above[half, dim])
-        value = jnp.where(place == 1, own[half, dim], value)
-        return jnp.where(place == 3, inflow[:, half * HALF : (half + 1) * HALF], value)
+        opened = inflow[:, half * HALF : (half + 1) * HALF]
+        return choose(place, below[half, dim], own[half, dim], above[half, dim], opened)
 
     positive = lax.axis_index("vel") >= NVX // 2
-    face = [places[:, k : k + 1] for k in range(6)]
-    face_x = jnp.where(positive, face[0], face[1])
     first = pl.multiple_of(jnp.where(positive, 0, (BS - 1) * GROUPS), GROUPS)
     kx = dt * jnp.abs(cx)
     ky = dt * jnp.abs(cy)
     kz = dt * jnp.abs(cz)
     sub = lax.broadcasted_iota(jnp.int32, (BS, HALF), 0)
-    one = jnp.ones_like(cy)
-    plane = cy * cy + cz * cz
-    table = weight * jnp.concatenate(
-        [one, cy, cz, cy * cy, cz * cz, cy * cz, cy * plane, cz * plane], axis=0
-    )
-    coarse = table.astype(jnp.bfloat16)
-    table = jnp.concatenate([coarse.astype(F32), table - coarse.astype(F32)], axis=0)
-    table = table.astype(jnp.bfloat16)
-    total = jnp.zeros((2 * BS, CELLS), F32)
     for half in range(2):
         lanes = slice(half * HALF, (half + 1) * HALF)
         _, edge = upwind_edge(cz[:, lanes], sub)
@@ -201,17 +306,6 @@
                 advected[half, at] = value
         rows = pl.ds(first, GROUPS)
         advected[half, rows] = advected[half, rows] + gx
-        value = advected[half]
-        high = value.astype(jnp.bfloat16)
-        low = (value - high.astype(F32)).astype(jnp.bfloat16)
-        for piece in (high, low):
-            total = total + lax.dot_general(
-                table[:, lanes],
-                piece,
-                (((1,), (1,)), ((), ())),
-                preferred_element_type=F32,
-            )
-    partial[...] = jnp.broadcast_to(total[:BS] + total[BS:], (NVX, BS, CELLS))
 
 
 def bfloat_pieces(value):
@@ -292,12 +386,13 @@
         first += chunk
 
 
-def collide_kernel(gathered, solid, advected, basis, filled, faces, turned):
+def collide_kernel(gathered, solid, advected, basis, filled, faces, flux, turned):
     def store(half, first, count, value):
         filled[half, first : first + count] = value
 
     collide(gathered, solid, advected, basis, turned, [PIECE] * PIECES, store)
     store_faces(filled, faces)
+    face_flux(faces, flux)
 
 
 def last_kernel(gathered, solid, advected, basis, result, turned, out, sems):
@@ -321,6 +416,10 @@
 FIELD = jax.ShapeDtypeStruct((2, CELLS, HALF), F32)
 RESULT = jax.ShapeDtypeStruct((CELLS, LANES), F32)
 FACES = jax.ShapeDtypeStruct((2, 3, GROUPS, HALF), F32)
+SPREAD = jax.ShapeDtypeStruct((6 * GROUPS, CELLS), jnp.bfloat16)
+FLUX = jax.ShapeDtypeStruct((3, BS, 2 * GROUPS), F32)
+LOCAL = jax.ShapeDtypeStruct((BS, CELLS), F32)
+SOLID = jax.ShapeDtypeStruct((1, CELLS), jnp.int32)
 PARTIAL = jax.ShapeDtypeStruct((NVX, BS, CELLS), F32)
 LAST_SIZES = (176, 160, 112, 64)
 BASIS = jax.ShapeDtypeStruct((3 * NVX, 3 * LANES), jnp.bfloat16)
@@ -346,37 +445,37 @@
     count = lax.axis_size("space")
     forward = [(i, (i + 1) % count) for i in range(count)]
     backward = [(target, source) for source, target in forward]
-    filled, faces = call(
+    filled, faces, flux, solid = call(
         fill_kernel,
         [HBM] * 2,
-        [FIELD, FACES],
-        [
-            pltpu.VMEM((CELLS, LANES), F32),
-            pltpu.VMEM((1, CELLS), jnp.int32),
-            pltpu.SemaphoreType.DMA((PIECES + 1,)),
-        ],
+        [FIELD, FACES, FLUX, SOLID],
+        [pltpu.VMEM((CELLS, LANES), F32), pltpu.SemaphoreType.DMA((2,))],
     )(
         pltpu.with_memory_space_constraint(dist[0], pltpu.HBM),
         pltpu.with_memory_space_constraint(solid, pltpu.HBM),
     )
     for step in range(ITERS):
+        flux_below = lax.ppermute(flux, "space", forward)
         below = lax.ppermute(faces, "space", forward)
+        flux_above = lax.ppermute(flux, "space", backward)
         above = lax.ppermute(faces, "space", backward)
         if step == 0:
-            inner, basis = call(inner_kernel, [VMEM], [FIELD, BASIS])(filled)
+            inner, local, basis, spread, open_flux = call(
+                first_inner_kernel, [VMEM], [FIELD, LOCAL, BASIS, SPREAD, FLUX]
+            )(filled)
         else:
-            (inner,) = call(inner_kernel, [VMEM], [FIELD])(filled)
-        advected, partial = call(
-            ghost_kernel,
-            [VMEM] * 5,
-            [FIELD, PARTIAL],
-            [pltpu.VMEM((2, GROUPS, HALF), F32)],
+            inner, local = call(inner_kernel, [VMEM], [FIELD, LOCAL])(filled)
+        (partial,) = call(join_kernel, [VMEM] * 7, [PARTIAL])(
+            neighbours, local, flux, flux_below, flux_above, open_flux, spread
+        )
+        gathered = lax.all_to_all(partial, "vel", 0, 0, tiled=True)
+        (advected,) = call(
+            ghost_kernel, [VMEM] * 5, [FIELD], [pltpu.VMEM((2, GROUPS, HALF), F32)]
         )(neighbours, inner, faces, below, above)
-        gathered = lax.all_to_all(partial, "vel", 0, 0, tiled=True)
         if step < ITERS - 1:
-            filled, faces = call(collide_kernel, [VMEM] * 4, [FIELD, FACES], [TURNED])(
-                gathered, solid, advected, basis
-            )
+            filled, faces, flux = call(
+                collide_kernel, [VMEM] * 4, [FIELD, FACES, FLUX], [TURNED]
+            )(gathered, solid, advected, basis)
         else:
             (filled,) = call(
                 last_kernel,

time: 60 us -> 60.2 us (level)
  blocking collectives: 26.2 us -> 0 us
  starting transfers between devices: 16.7 us -> 31.7 us
  waiting for transfers between devices: 11.7 us -> 20.4 us
  Pallas kernels: 4.4 us -> 7 us
    all_to_all x2 -> x0, blocking collectives: 26.2 us -> none  [on_device(): gathered = lax.all_to_all(partial, 'vel', 0, 0, tiled=True)]
    ppermute x0 -> x4, starting transfers between devices: none -> 16.7 us  [the longest x2 16.2 us: on_device(): flux_above = lax.ppermute(flux, 'space', backward)]
    ppermute x2, starting transfers between devices: 16.2 us -> 0.01 us  [on_device(): above = lax.ppermute(faces, 'space', backward)]
    all_to_all x0 -> x2, starting transfers between devices: none -> 13.9 us  [on_device(): gathered = lax.all_to_all(partial, 'vel', 0, 0, tiled=True)]
    ppermute x0 -> x4, waiting for transfers between devices: none -> 7.17 us  [the longest x2 5.85 us: on_device(): flux_below = lax.ppermute(flux, 'space', forward)]
    pallas_call x6 -> x8, Pallas kernels: 3.14 us -> 5.75 us  [the longest x2 2.06 us: on_device(): call(join_kernel, [VMEM] * 7, [PARTIAL])]
    all_to_all x0 -> x2, waiting for transfers between devices: none -> 1.61 us  [on_device(): gathered = lax.all_to_all(partial, 'vel', 0, 0, tiled=True)]
  transfers between devices with their start and end apart: 4 -> 10, of which waited for: 4 -> 10; matrix products, arithmetic and copies ran while one was open for 0% -> 0% of each run, Pallas kernels for 1% -> 2%
where the time goes in v4:
time: 60.2 us; the launch traced here: 59.8 us
  starting transfers between devices  31.7 us (53%)
  waiting for transfers between devices  20.4 us (34%)
  Pallas kernels  7 us (12%)
  local copies, waits for them, and re-layouts  0.66 us (1%)
    ppermute x2, starting transfers between devices, on_device(): flux_above = lax.ppermute(flux, 'space', backward)  16.2 us
    all_to_all x2, starting transfers between devices, on_device(): gathered = lax.all_to_all(partial, 'vel', 0, 0, tiled=True)  13.9 us
    ppermute x2, waiting for transfers between devices, on_device(): below = lax.ppermute(faces, 'space', forward)  6.27 us
    ppermute x2, waiting for transfers between devices, on_device(): flux_below = lax.ppermute(flux, 'space', forward)  5.85 us
    ppermute x2, waiting for transfers between devices, on_device(): above = lax.ppermute(faces, 'space', backward)  5.36 us
    pallas_call x2, Pallas kernels, on_device(): call(join_kernel, [VMEM] * 7, [PARTIAL])  2.06 us
    all_to_all x2, waiting for transfers between devices, on_device(): gathered = lax.all_to_all(partial, 'vel', 0, 0, tiled=True)  1.61 us
    pallas_call x1, Pallas kernels, on_device(): call(fill_kernel, [HBM] * 2, [FIELD, FACES, FLUX, SOLID], [pltpu.VMEM((CE...  1.44 us
  transfers between devices with their start and end apart: 10, of which 10 were waited for; matrix products, arithmetic and copies ran while one was open for 0% of the time, Pallas kernels for 2%

profile of v4, /device:TPU:2, one launch (start us, length us, event | category | flops | bytes accessed | tf_op | source)
XLA Modules:
  0.0 59.8 jit_solution(11204691560558415192)
XLA Ops:
  0.0 1.4 %shard_map.37 = (f32[2,512,128]{2,1,0:T(8,128)S(1)}, f32[2,3,64,128]{3,2,1,0:T(8,128)S(1)}, f32[3,8,128]{2,1,0:T(8,128)S(1)}, s32[1,512]{1,0:T(1,128)S(1)}) custom-call(f32[512,256]{1,0:T(8,128)} %bitcast.2, s32[1,512]{1,0:T(1,128)} %solid_hbm.1), custom_call_target="tpu_custom_call" | custom-call | flops 5242880 | bytes 1048576 | tf_op jit(solution)/shard_map/pallas_call | solution.py:448
  1.5 16.2 %collective-permute-start.1 = (f32[3,8,128]{2,1,0:T(8,128)S(1)}, f32[3,8,128]{2,1,0:T(8,128)S(1)}, u32[]{:S(2)}, u32[]{:S(2)}) collective-permute-start(f32[3,8,128]{2,1,0:T(8,128)S(1)} %get-tuple-element.21.own), channel_id=1, source_target_pairs={{16,0},{32,16},{48,32},{64,48},{80,64},{96,80},{112,96},{128,112},... | collective-permute-start | bytes 36872 | tf_op jit(solution)/shard_map/ppermute | solution.py:460
  17.7 0.6 shard_map.38
  18.3 0.8 %collective-permute-done.1.above = f32[3,8,128]{2,1,0:T(8,128)S(1)} collective-permute-done((f32[3,8,128]{2,1,0:T(8,128)S(1)}, f32[3,8,128]{2,1,0:T(8,128)S(1)}, u32[]{:S(2)}, u32[]{:S(2)}) %collective-permute-start.1) | collective-permute-done | bytes 12320 | tf_op jit(solution)/shard_map/ppermute | solution.py:460
  19.1 2.9 %collective-permute-done.below = f32[3,8,128]{2,1,0:T(8,128)S(1)} collective-permute-done((f32[3,8,128]{2,1,0:T(8,128)S(1)}, f32[3,8,128]{2,1,0:T(8,128)S(1)}, u32[]{:S(2)}, u32[]{:S(2)}) %collective-permute-start) | collective-permute-done | bytes 12320 | tf_op jit(solution)/shard_map/ppermute | solution.py:458
  22.0 0.7 %copy-done = s32[1,6]{1,0:T(1,128)S(1)} copy-done((s32[1,6]{1,0:T(1,128)S(1)}, s32[1,6]{1,0:T(1,128)}, u32[]{:S(2)}) %copy-start) | copy-done | bytes 48
  22.7 1.0 %shard_map.39 = f32[16,8,512]{2,1,0:T(8,128)} custom-call(s32[1,6]{1,0:T(1,128)S(1)} %copy-done, f32[8,512]{1,0:T(8,128)S(1)} %get-tuple-element.20.local, f32[3,8,128]{2,1,0:T(8,128)S(1)} %get-tuple-element.21.own, f32[3,8,128]{2,1,0:T(8,128)S(1)} %collective-permute-done.below, f32[3,8,128]{2,1,0:T(8,128)S(1)} %collective-permute-done.1.above, ...), custom_call_target="tpu_custom_call" | custom-call | flops 5242880 | bytes 1048576 | tf_op jit(solution)/shard_map/pallas_call | solution.py:468
  23.7 7.5 %all-to-all-start = ((f32[16,8,512]{2,1,0:T(8,128)}), f32[16,8,512]{2,1,0:T(8,128)S(1)}, u32[]{:S(2)}, u32[]{:S(2)}) async-start(f32[16,8,512]{2,1,0:T(8,128)} %shard_map.39), calls=%async_computation | async-start | bytes 524288 | tf_op jit(solution)/shard_map/all_to_all | solution.py:471
  31.2 0.5 collective-permute-start.2
  31.7 2.7 %collective-permute-done.3.above = f32[2,3,64,128]{3,2,1,0:T(8,128)S(1)} collective-permute-done((f32[2,3,64,128]{3,2,1,0:T(8,128)S(1)}, f32[2,3,64,128]{3,2,1,0:T(8,128)S(1)}, u32[]{:S(2)}, u32[]{:S(2)}) %collective-permute-start.3) | collective-permute-done | bytes 196640 | tf_op jit(solution)/shard_map/ppermute | solution.py:461
  34.4 3.1 %collective-permute-done.2.below = f32[2,3,64,128]{3,2,1,0:T(8,128)S(1)} collective-permute-done((f32[2,3,64,128]{3,2,1,0:T(8,128)S(1)}, f32[2,3,64,128]{3,2,1,0:T(8,128)S(1)}, u32[]{:S(2)}, u32[]{:S(2)}) %collective-permute-start.2) | collective-permute-done | bytes 196640 | tf_op jit(solution)/shard_map/ppermute | solution.py:459
  37.7 0.8 %all-to-all-done.gathered = f32[16,8,512]{2,1,0:T(8,128)S(1)} async-done(((f32[16,8,512]{2,1,0:T(8,128)}), f32[16,8,512]{2,1,0:T(8,128)S(1)}, u32[]{:S(2)}, u32[]{:S(2)}) %all-to-all-start) | async-done | bytes 262176 | tf_op jit(solution)/shard_map/all_to_all | solution.py:471
  38.5 0.9 %shard_map.41 = (f32[2,512,128]{2,1,0:T(8,128)S(1)}, f32[2,3,64,128]{3,2,1,0:T(8,128)S(1)}, f32[3,8,128]{2,1,0:T(8,128)S(1)}) custom-call(f32[16,8,512]{2,1,0:T(8,128)S(1)} %all-to-all-done.gathered, s32[1,512]{1,0:T(1,128)S(1)} %get-tuple-element.24.solid, f32[2,512,128]{2,1,0:T(8,128)S(1)} %shard_map.40.advected, bf16[48,768]{1,0:T(8,128)(2,1)S(1)} %get-tuple-element.27.basis), custom_call_target="tpu_custom_call" | custom-call | flops 5242880 | bytes 1048576 | tf_op jit(solution)/shard_map/pallas_call | solution.py:476
  39.4 0.5 collective-permute-start.4
  39.9 0.4 shard_map.42
  40.3 0.5 collective-permute-done.5.above
  40.8 2.9 %collective-permute-done.4.below = f32[3,8,128]{2,1,0:T(8,128)S(1)} collective-permute-done((f32[3,8,128]{2,1,0:T(8,128)S(1)}, f32[3,8,128]{2,1,0:T(8,128)S(1)}, u32[]{:S(2)}, u32[]{:S(2)}) %collective-permute-start.4) | collective-permute-done | bytes 12320 | tf_op jit(solution)/shard_map/ppermute | solution.py:458
  43.7 1.0 %shard_map.43 = f32[16,8,512]{2,1,0:T(8,128)} custom-call(s32[1,6]{1,0:T(1,128)S(1)} %copy-done, f32[8,512]{1,0:T(8,128)S(1)} %get-tuple-element.29.local, f32[3,8,128]{2,1,0:T(8,128)S(1)} %get-tuple-element.30.own, f32[3,8,128]{2,1,0:T(8,128)S(1)} %collective-permute-done.4.below, f32[3,8,128]{2,1,0:T(8,128)S(1)} %collective-permute-done.5.above, ...), custom_call_target="tpu_custom_call" | custom-call | flops 5242880 | bytes 1048576 | tf_op jit(solution)/shard_map/pallas_call | solution.py:468
  44.7 6.4 %all-to-all-start.1 = ((f32[16,8,512]{2,1,0:T(8,128)}), f32[16,8,512]{2,1,0:T(8,128)S(1)}, u32[]{:S(2)}, u32[]{:S(2)}) async-start(f32[16,8,512]{2,1,0:T(8,128)} %shard_map.43), calls=%async_computation.1 | async-start | bytes 524288 | tf_op jit(solution)/shard_map/all_to_all | solution.py:471
  51.2 0.5 collective-permute-start.6
  51.7 2.7 %collective-permute-done.7.above = f32[2,3,64,128]{3,2,1,0:T(8,128)S(1)} collective-permute-done((f32[2,3,64,128]{3,2,1,0:T(8,128)S(1)}, f32[2,3,64,128]{3,2,1,0:T(8,128)S(1)}, u32[]{:S(2)}, u32[]{:S(2)}) %collective-permute-start.7) | collective-permute-done | bytes 196640 | tf_op jit(solution)/shard_map/ppermute | solution.py:461
  54.4 3.1 %collective-permute-done.6.below = f32[2,3,64,128]{3,2,1,0:T(8,128)S(1)} collective-permute-done((f32[2,3,64,128]{3,2,1,0:T(8,128)S(1)}, f32[2,3,64,128]{3,2,1,0:T(8,128)S(1)}, u32[]{:S(2)}, u32[]{:S(2)}) %collective-permute-start.6) | collective-permute-done | bytes 196640 | tf_op jit(solution)/shard_map/ppermute | solution.py:459
  57.7 0.8 %all-to-all-done.1.gathered = f32[16,8,512]{2,1,0:T(8,128)S(1)} async-done(((f32[16,8,512]{2,1,0:T(8,128)}), f32[16,8,512]{2,1,0:T(8,128)S(1)}, u32[]{:S(2)}, u32[]{:S(2)}) %all-to-all-start.1) | async-done | bytes 262176 | tf_op jit(solution)/shard_map/all_to_all | solution.py:471
  58.5 1.3 %shard_map.45 = f32[512,256]{1,0:T(8,128)} custom-call(f32[16,8,512]{2,1,0:T(8,128)S(1)} %all-to-all-done.1.gathered, s32[1,512]{1,0:T(1,128)S(1)} %get-tuple-element.24.solid, f32[2,512,128]{2,1,0:T(8,128)S(1)} %shard_map.44.advected, bf16[48,768]{1,0:T(8,128)(2,1)S(1)} %get-tuple-element.27.basis), custom_call_target="tpu_custom_call" | custom-call | flops 5242880 | bytes 1048576 | tf_op jit(solution)/shard_map/pallas_call | solution.py:480
  (7 shorter events, 0.4 us)
Async XLA Ops:
  1.5 17.6 %collective-permute-start.1 = (f32[3,8,128]{2,1,0:T(8,128)S(1)}, f32[3,8,128]{2,1,0:T(8,128)S(1)}, u32[]{:S(2)}, u32[]{:S(2)}) collective-permute-start(f32[3,8,128]{2,1,0:T(8,128)S(1)} %get-tuple-element.21.own), channel_id=1, source_target_pairs={{16,0},{32,16},{48,32},{64,48},{80,64},{96,80},{112,96},{128,112},... | collective-permute-start | bytes 36872 | tf_op jit(solution)/shard_map/ppermute | solution.py:460
  17.7 4.3 %collective-permute-start = (f32[3,8,128]{2,1,0:T(8,128)S(1)}, f32[3,8,128]{2,1,0:T(8,128)S(1)}, u32[]{:S(2)}, u32[]{:S(2)}) collective-permute-start(f32[3,8,128]{2,1,0:T(8,128)S(1)} %get-tuple-element.21.own), channel_id=1, source_target_pairs={{0,16},{16,32},{32,48},{48,64},{64,80},{80,96},{96,112},{112,128},... | collective-permute-start | bytes 36872 | tf_op jit(solution)/shard_map/ppermute | solution.py:458
  22.0 0.7 %copy-start = (s32[1,6]{1,0:T(1,128)S(1)}, s32[1,6]{1,0:T(1,128)}, u32[]{:S(2)}) copy-start(s32[1,6]{1,0:T(1,128)} %neighbours.7) | copy-start | bytes 76
  23.7 14.8 %all-to-all-start = ((f32[16,8,512]{2,1,0:T(8,128)}), f32[16,8,512]{2,1,0:T(8,128)S(1)}, u32[]{:S(2)}, u32[]{:S(2)}) async-start(f32[16,8,512]{2,1,0:T(8,128)} %shard_map.39), calls=%async_computation | async-start | bytes 524288 | tf_op jit(solution)/shard_map/all_to_all | solution.py:471
  31.2 3.2 %collective-permute-start.3 = (f32[2,3,64,128]{3,2,1,0:T(8,128)S(1)}, f32[2,3,64,128]{3,2,1,0:T(8,128)S(1)}, u32[]{:S(2)}, u32[]{:S(2)}) collective-permute-start(f32[2,3,64,128]{3,2,1,0:T(8,128)S(1)} %get-tuple-element.26.own), channel_id=1, source_target_pairs={{16,0},{32,16},{48,32},{64,48},{80,64},{96,80},{112,96},{128,112},... | collective-permute-start | bytes 589832 | tf_op jit(solution)/shard_map/ppermute | solution.py:461
  31.2 6.3 %collective-permute-start.2 = (f32[2,3,64,128]{3,2,1,0:T(8,128)S(1)}, f32[2,3,64,128]{3,2,1,0:T(8,128)S(1)}, u32[]{:S(2)}, u32[]{:S(2)}) collective-permute-start(f32[2,3,64,128]{3,2,1,0:T(8,128)S(1)} %get-tuple-element.26.own), channel_id=1, source_target_pairs={{0,16},{16,32},{32,48},{48,64},{64,80},{80,96},{96,112},{112,128},... | collective-permute-start | bytes 589832 | tf_op jit(solution)/shard_map/ppermute | solution.py:459
  39.4 1.4 %collective-permute-start.5 = (f32[3,8,128]{2,1,0:T(8,128)S(1)}, f32[3,8,128]{2,1,0:T(8,128)S(1)}, u32[]{:S(2)}, u32[]{:S(2)}) collective-permute-start(f32[3,8,128]{2,1,0:T(8,128)S(1)} %get-tuple-element.30.own), channel_id=1, source_target_pairs={{16,0},{32,16},{48,32},{64,48},{80,64},{96,80},{112,96},{128,112},... | collective-permute-start | bytes 36872 | tf_op jit(solution)/shard_map/ppermute | solution.py:460
  39.4 4.3 %collective-permute-start.4 = (f32[3,8,128]{2,1,0:T(8,128)S(1)}, f32[3,8,128]{2,1,0:T(8,128)S(1)}, u32[]{:S(2)}, u32[]{:S(2)}) collective-permute-start(f32[3,8,128]{2,1,0:T(8,128)S(1)} %get-tuple-element.30.own), channel_id=1, source_target_pairs={{0,16},{16,32},{32,48},{48,64},{64,80},{80,96},{96,112},{112,128},... | collective-permute-start | bytes 36872 | tf_op jit(solution)/shard_map/ppermute | solution.py:458
  44.7 13.8 %all-to-all-start.1 = ((f32[16,8,512]{2,1,0:T(8,128)}), f32[16,8,512]{2,1,0:T(8,128)S(1)}, u32[]{:S(2)}, u32[]{:S(2)}) async-start(f32[16,8,512]{2,1,0:T(8,128)} %shard_map.43), calls=%async_computation.1 | async-start | bytes 524288 | tf_op jit(solution)/shard_map/all_to_all | solution.py:471
  51.2 3.2 %collective-permute-start.7 = (f32[2,3,64,128]{3,2,1,0:T(8,128)S(1)}, f32[2,3,64,128]{3,2,1,0:T(8,128)S(1)}, u32[]{:S(2)}, u32[]{:S(2)}) collective-permute-start(f32[2,3,64,128]{3,2,1,0:T(8,128)S(1)} %get-tuple-element.32.own), channel_id=1, source_target_pairs={{16,0},{32,16},{48,32},{64,48},{80,64},{96,80},{112,96},{128,112},... | collective-permute-start | bytes 589832 | tf_op jit(solution)/shard_map/ppermute | solution.py:461
  51.2 6.3 %collective-permute-start.6 = (f32[2,3,64,128]{3,2,1,0:T(8,128)S(1)}, f32[2,3,64,128]{3,2,1,0:T(8,128)S(1)}, u32[]{:S(2)}, u32[]{:S(2)}) collective-permute-start(f32[2,3,64,128]{3,2,1,0:T(8,128)S(1)} %get-tuple-element.32.own), channel_id=1, source_target_pairs={{0,16},{16,32},{32,48},{48,64},{64,80},{80,96},{96,112},{112,128},... | collective-permute-start | bytes 589832 | tf_op jit(solution)/shard_map/ppermute | solution.py:459

commit v5 on v4

--- a/solution.py
+++ b/solution.py
@@ -124,10 +124,13 @@
     flux_moments(lambda half, dim: faces[half, dim], flux)
 
 
-def fill_kernel(dist_hbm, solid_hbm, filled, faces, flux, solid, dist, sems):
+def fill_kernel(
+    dist_hbm, solid_hbm, table_hbm, filled, faces, flux, solid, neighbours, dist, sems
+):
     copies = [
         pltpu.make_async_copy(solid_hbm, solid, sems.at[0]),
         pltpu.make_async_copy(dist_hbm, dist, sems.at[1]),
+        pltpu.make_async_copy(table_hbm, neighbours, sems.at[2]),
     ]
     for copy in copies:
         copy.start()
@@ -147,6 +150,7 @@
         filled[half] = jnp.where(inside, wall[:, lanes], dist[:, lanes])
     store_faces(filled, faces)
     face_flux(faces, flux)
+    copies[2].wait()
 
 
 def upwind_edge(cz, sub):
@@ -270,7 +274,7 @@
     partial[...] = jnp.broadcast_to(total, (NVX, BS, CELLS))
 
 
-def ghost_kernel(neighbours, inner, own, below, above, advected, ghost_z):
+def add_ghosts(neighbours, inner, own, below, above, advected, ghost_z):
     cx = own_cx()
     cy, cz = lane_velocities()
     inflow = maxwellian(20.0, 2.5, 1.0, cx, cy, cz)
@@ -317,7 +321,7 @@
     return pieces
 
 
-def collide(gathered, solid, advected, basis, turned, sizes, store):
+def coefficient_kernel(gathered, solid, turned):
     sums = [None] * 4
     for a in range(NVX // 2, NVX):
         ca = (a - centre) * velocity_step
@@ -371,6 +375,9 @@
     rows = rows + [jnp.zeros_like(rho)] * (NVX - len(rows))
     pieces = jnp.concatenate(bfloat_pieces(jnp.concatenate(rows, axis=0)), axis=0)
     turned[...] = pieces.T.astype(jnp.bfloat16)
+
+
+def collide(turned, basis, advected, sizes, store):
     first = 0
     for chunk in sizes:
         at = slice(first, first + chunk)
@@ -386,16 +393,21 @@
         first += chunk
 
 
-def collide_kernel(gathered, solid, advected, basis, filled, faces, flux, turned):
+def collide_kernel(
+    turned, basis, neighbours, inner, own, below, above, filled, faces, flux, advected, ghost_z
+):
     def store(half, first, count, value):
         filled[half, first : first + count] = value
 
-    collide(gathered, solid, advected, basis, turned, [PIECE] * PIECES, store)
+    add_ghosts(neighbours, inner, own, below, above, advected, ghost_z)
+    collide(turned, basis, advected, [PIECE] * PIECES, store)
     store_faces(filled, faces)
     face_flux(faces, flux)
 
 
-def last_kernel(gathered, solid, advected, basis, result, turned, out, sems):
+def last_kernel(
+    turned, basis, neighbours, inner, own, below, above, result, advected, ghost_z, out, sems
+):
     copies = []
 
     def store(half, first, count, value):
@@ -406,7 +418,8 @@
             copy.start()
             copies.append(copy)
 
-    collide(gathered, solid, advected, basis, turned, LAST_SIZES, store)
+    add_ghosts(neighbours, inner, own, below, above, advected, ghost_z)
+    collide(turned, basis, advected, LAST_SIZES, store)
     for copy in copies:
         copy.wait()
 
@@ -420,10 +433,11 @@
 FLUX = jax.ShapeDtypeStruct((3, BS, 2 * GROUPS), F32)
 LOCAL = jax.ShapeDtypeStruct((BS, CELLS), F32)
 SOLID = jax.ShapeDtypeStruct((1, CELLS), jnp.int32)
+TABLE = jax.ShapeDtypeStruct((1, 6), jnp.int32)
 PARTIAL = jax.ShapeDtypeStruct((NVX, BS, CELLS), F32)
 LAST_SIZES = (176, 160, 112, 64)
 BASIS = jax.ShapeDtypeStruct((3 * NVX, 3 * LANES), jnp.bfloat16)
-TURNED = pltpu.VMEM((CELLS, 3 * NVX), jnp.bfloat16)
+TURNED = jax.ShapeDtypeStruct((CELLS, 3 * NVX), jnp.bfloat16)
 
 
 def call(kernel, ins, outs, scratch=(), out_spec=VMEM):
@@ -445,14 +459,15 @@
     count = lax.axis_size("space")
     forward = [(i, (i + 1) % count) for i in range(count)]
     backward = [(target, source) for source, target in forward]
-    filled, faces, flux, solid = call(
+    filled, faces, flux, solid, neighbours = call(
         fill_kernel,
-        [HBM] * 2,
-        [FIELD, FACES, FLUX, SOLID],
-        [pltpu.VMEM((CELLS, LANES), F32), pltpu.SemaphoreType.DMA((2,))],
+        [HBM] * 3,
+        [FIELD, FACES, FLUX, SOLID, TABLE],
+        [pltpu.VMEM((CELLS, LANES), F32), pltpu.SemaphoreType.DMA((3,))],
     )(
         pltpu.with_memory_space_constraint(dist[0], pltpu.HBM),
         pltpu.with_memory_space_constraint(solid, pltpu.HBM),
+        pltpu.with_memory_space_constraint(neighbours, pltpu.HBM),
     )
     for step in range(ITERS):
         flux_below = lax.ppermute(flux, "space", forward)
@@ -469,21 +484,16 @@
             neighbours, local, flux, flux_below, flux_above, open_flux, spread
         )
         gathered = lax.all_to_all(partial, "vel", 0, 0, tiled=True)
-        (advected,) = call(
-            ghost_kernel, [VMEM] * 5, [FIELD], [pltpu.VMEM((2, GROUPS, HALF), F32)]
-        )(neighbours, inner, faces, below, above)
+        (turned,) = call(coefficient_kernel, [VMEM] * 2, [TURNED])(gathered, solid)
+        operands = (turned, basis, neighbours, inner, faces, below, above)
+        room = [pltpu.VMEM((2, CELLS, HALF), F32), pltpu.VMEM((2, GROUPS, HALF), F32)]
         if step < ITERS - 1:
-            filled, faces, flux = call(
-                collide_kernel, [VMEM] * 4, [FIELD, FACES, FLUX], [TURNED]
-            )(gathered, solid, advected, basis)
+            filled, faces, flux = call(collide_kernel, [VMEM] * 7, [FIELD, FACES, FLUX], room)(
+                *operands
+            )
         else:
-            (filled,) = call(
-                last_kernel,
-                [VMEM] * 4,
-                [RESULT],
-                [TURNED, pltpu.VMEM((CELLS, LANES), F32), pltpu.SemaphoreType.DMA((4,))],
-                HBM,
-            )(gathered, solid, advected, basis)
+            room = room + [pltpu.VMEM((CELLS, LANES), F32), pltpu.SemaphoreType.DMA((4,))]
+            (filled,) = call(last_kernel, [VMEM] * 7, [RESULT], room, HBM)(*operands)
     return filled[None]
 
 

time: 60.2 us -> 59.3 us (0.985)
  local copies, waits for them, and re-layouts: 0.66 us -> 0 us
    all_to_all x2, waiting for transfers between devices: 1.61 us -> 13.6 us  [on_device(): gathered = lax.all_to_all(partial, 'vel', 0, 0, tiled=True)]
    ppermute x2, waiting for transfers between devices: 6.27 us -> 0.01 us  [on_device(): below = lax.ppermute(faces, 'space', forward)]
    ppermute x2, waiting for transfers between devices: 5.36 us -> 0.01 us  [on_device(): above = lax.ppermute(faces, 'space', backward)]
    unnamed x2 -> x0, local copies, waits for them, and re-layouts: 0.66 us -> none
  transfers between devices with their start and end apart: 10 -> 10, of which waited for: 10 -> 6; matrix products, arithmetic and copies ran while one was open for 0% -> 0% of each run, Pallas kernels for 2% -> 2%
where the time goes in v5:
time: 59.3 us; the launch traced here: 58.9 us
  starting transfers between devices  31.2 us (53%)
  waiting for transfers between devices  20.8 us (35%)
  Pallas kernels  6.8 us (11%)
    ppermute x2, starting transfers between devices, on_device(): flux_above = lax.ppermute(flux, 'space', backward)  16.2 us
    all_to_all x2, waiting for transfers between devices, on_device(): gathered = lax.all_to_all(partial, 'vel', 0, 0, tiled=True)  13.6 us
    all_to_all x2, starting transfers between devices, on_device(): gathered = lax.all_to_all(partial, 'vel', 0, 0, tiled=True)  13.4 us
    ppermute x2, waiting for transfers between devices, on_device(): flux_below = lax.ppermute(flux, 'space', forward)  5.85 us
    pallas_call x2, Pallas kernels, on_device(): call(join_kernel, [VMEM] * 7, [PARTIAL])  2.06 us
    pallas_call x1, Pallas kernels, on_device(): call(fill_kernel, [HBM] * 3, [FIELD, FACES, FLUX, SOLID, TABLE], [pltpu.V...  1.45 us
    ppermute x2, waiting for transfers between devices, on_device(): flux_above = lax.ppermute(flux, 'space', backward)  1.32 us
  transfers between devices with their start and end apart: 10, of which 6 were waited for; matrix products, arithmetic and copies ran while one was open for 0% of the time, Pallas kernels for 2%

profile of v5, /device:TPU:2, one launch (start us, length us, event | category | flops | bytes accessed | tf_op | source)
XLA Modules:
  0.0 58.9 jit_solution(4640722530646286868)
XLA Ops:
  0.0 1.5 %shard_map.37 = (f32[2,512,128]{2,1,0:T(8,128)S(1)}, f32[2,3,64,128]{3,2,1,0:T(8,128)S(1)}, f32[3,8,128]{2,1,0:T(8,128)S(1)}, s32[1,512]{1,0:T(1,128)S(1)}, s32[1,6]{1,0:T(1,128)S(1)}) custom-call(f32[512,256]{1,0:T(8,128)} %bitcast.2, s32[1,512]{1,0:T(1,128)} %solid_hbm.1, s32[1,6]{1,0:T(1,128)} %table_hbm.1), custom_call_target="tpu_custom_call" | custom-call | flops 5242880 | bytes 1048576 | tf_op jit(solution)/shard_map/pallas_call | solution.py:462
  1.5 16.2 %collective-permute-start.1 = (f32[3,8,128]{2,1,0:T(8,128)S(1)}, f32[3,8,128]{2,1,0:T(8,128)S(1)}, u32[]{:S(2)}, u32[]{:S(2)}) collective-permute-start(f32[3,8,128]{2,1,0:T(8,128)S(1)} %get-tuple-element.23.own), channel_id=1, source_target_pairs={{16,0},{32,16},{48,32},{64,48},{80,64},{96,80},{112,96},{128,112},... | collective-permute-start | bytes 36872 | tf_op jit(solution)/shard_map/ppermute | solution.py:475
  17.7 0.6 shard_map.38
  18.3 0.8 %collective-permute-done.1.above = f32[3,8,128]{2,1,0:T(8,128)S(1)} collective-permute-done((f32[3,8,128]{2,1,0:T(8,128)S(1)}, f32[3,8,128]{2,1,0:T(8,128)S(1)}, u32[]{:S(2)}, u32[]{:S(2)}) %collective-permute-start.1) | collective-permute-done | bytes 12320 | tf_op jit(solution)/shard_map/ppermute | solution.py:475
  19.1 2.9 %collective-permute-done.below = f32[3,8,128]{2,1,0:T(8,128)S(1)} collective-permute-done((f32[3,8,128]{2,1,0:T(8,128)S(1)}, f32[3,8,128]{2,1,0:T(8,128)S(1)}, u32[]{:S(2)}, u32[]{:S(2)}) %collective-permute-start) | collective-permute-done | bytes 12320 | tf_op jit(solution)/shard_map/ppermute | solution.py:473
  22.0 1.0 %shard_map.39 = f32[16,8,512]{2,1,0:T(8,128)} custom-call(s32[1,6]{1,0:T(1,128)S(1)} %get-tuple-element.20.neighbours, f32[8,512]{1,0:T(8,128)S(1)} %get-tuple-element.22.local, f32[3,8,128]{2,1,0:T(8,128)S(1)} %get-tuple-element.23.own, f32[3,8,128]{2,1,0:T(8,128)S(1)} %collective-permute-done.below, f32[3,8,128]{2,1,0:T(8,128)S(1)} %collective-permute-done.1.above, ...), custom_call_target="tpu_custom_call" | custom-call | flops 5242880 | bytes 1048576 | tf_op jit(solution)/shard_map/pallas_call | solution.py:483
  23.0 7.5 %all-to-all-start = ((f32[16,8,512]{2,1,0:T(8,128)}), f32[16,8,512]{2,1,0:T(8,128)S(1)}, u32[]{:S(2)}, u32[]{:S(2)}) async-start(f32[16,8,512]{2,1,0:T(8,128)} %shard_map.39), calls=%async_computation | async-start | bytes 524288 | tf_op jit(solution)/shard_map/all_to_all | solution.py:486
  30.5 0.5 collective-permute-start.2
  31.0 6.8 %all-to-all-done.gathered = f32[16,8,512]{2,1,0:T(8,128)S(1)} async-done(((f32[16,8,512]{2,1,0:T(8,128)}), f32[16,8,512]{2,1,0:T(8,128)S(1)}, u32[]{:S(2)}, u32[]{:S(2)}) %all-to-all-start) | async-done | bytes 262176 | tf_op jit(solution)/shard_map/all_to_all | solution.py:486
  37.9 0.2 shard_map.40.turned
  38.1 0.0 collective-permute-done.3.above
  38.1 0.7 %shard_map.41 = (f32[2,512,128]{2,1,0:T(8,128)S(1)}, f32[2,3,64,128]{3,2,1,0:T(8,128)S(1)}, f32[3,8,128]{2,1,0:T(8,128)S(1)}) custom-call(bf16[512,48]{1,0:T(8,128)(2,1)S(1)} %shard_map.40.turned, bf16[48,768]{1,0:T(8,128)(2,1)S(1)} %get-tuple-element.27.basis, s32[1,6]{1,0:T(1,128)S(1)} %get-tuple-element.20.neighbours, ...), custom_call_target="tpu_custom_call" | custom-call | flops 5242880 | bytes 1048576 | tf_op jit(solution)/shard_map/pallas_call | solution.py:491
  38.9 0.5 collective-permute-start.4
  39.4 0.4 shard_map.42
  39.8 0.5 collective-permute-done.5.above
  40.3 2.9 %collective-permute-done.4.below = f32[3,8,128]{2,1,0:T(8,128)S(1)} collective-permute-done((f32[3,8,128]{2,1,0:T(8,128)S(1)}, f32[3,8,128]{2,1,0:T(8,128)S(1)}, u32[]{:S(2)}, u32[]{:S(2)}) %collective-permute-start.4) | collective-permute-done | bytes 12320 | tf_op jit(solution)/shard_map/ppermute | solution.py:473
  43.2 1.0 %shard_map.43 = f32[16,8,512]{2,1,0:T(8,128)} custom-call(s32[1,6]{1,0:T(1,128)S(1)} %get-tuple-element.20.neighbours, f32[8,512]{1,0:T(8,128)S(1)} %get-tuple-element.31.local, f32[3,8,128]{2,1,0:T(8,128)S(1)} %get-tuple-element.32.own, f32[3,8,128]{2,1,0:T(8,128)S(1)} %collective-permute-done.4.below, f32[3,8,128]{2,1,0:T(8,128)S(1)} %collective-permute-done.5.above, ...), custom_call_target="tpu_custom_call" | custom-call | flops 5242880 | bytes 1048576 | tf_op jit(solution)/shard_map/pallas_call | solution.py:483
  44.2 6.0 %all-to-all-start.1 = ((f32[16,8,512]{2,1,0:T(8,128)}), f32[16,8,512]{2,1,0:T(8,128)S(1)}, u32[]{:S(2)}, u32[]{:S(2)}) async-start(f32[16,8,512]{2,1,0:T(8,128)} %shard_map.43), calls=%async_computation.1 | async-start | bytes 524288 | tf_op jit(solution)/shard_map/all_to_all | solution.py:486
  50.2 0.5 collective-permute-start.6
  50.7 6.8 %all-to-all-done.1.gathered = f32[16,8,512]{2,1,0:T(8,128)S(1)} async-done(((f32[16,8,512]{2,1,0:T(8,128)}), f32[16,8,512]{2,1,0:T(8,128)S(1)}, u32[]{:S(2)}, u32[]{:S(2)}) %all-to-all-start.1) | async-done | bytes 262176 | tf_op jit(solution)/shard_map/all_to_all | solution.py:486
  57.5 0.2 shard_map.44.turned
  57.8 0.0 collective-permute-done.7.above
  57.8 0.0 collective-permute-done.6.below
  57.8 1.1 %shard_map.45 = f32[512,256]{1,0:T(8,128)} custom-call(bf16[512,48]{1,0:T(8,128)(2,1)S(1)} %shard_map.44.turned, bf16[48,768]{1,0:T(8,128)(2,1)S(1)} %get-tuple-element.27.basis, s32[1,6]{1,0:T(1,128)S(1)} %get-tuple-element.20.neighbours, f32[2,512,128]{2,1,0:T(8,128)S(1)} %get-tuple-element.33.inner, f32[2,3,64,128]{3,2,1,0:T(8,128)S(1)} %get-tuple-element.34.own, ...), custom_call_target="tpu_custom_call" | custom-call | flops 5242880 | bytes 1048576 | tf_op jit(solution)/shard_map/pallas_call | solution.py:496
  (5 shorter events, 0.0 us)
Async XLA Ops:
  1.5 17.6 %collective-permute-start.1 = (f32[3,8,128]{2,1,0:T(8,128)S(1)}, f32[3,8,128]{2,1,0:T(8,128)S(1)}, u32[]{:S(2)}, u32[]{:S(2)}) collective-permute-start(f32[3,8,128]{2,1,0:T(8,128)S(1)} %get-tuple-element.23.own), channel_id=1, source_target_pairs={{16,0},{32,16},{48,32},{64,48},{80,64},{96,80},{112,96},{128,112},... | collective-permute-start | bytes 36872 | tf_op jit(solution)/shard_map/ppermute | solution.py:475
  17.7 4.3 %collective-permute-start = (f32[3,8,128]{2,1,0:T(8,128)S(1)}, f32[3,8,128]{2,1,0:T(8,128)S(1)}, u32[]{:S(2)}, u32[]{:S(2)}) collective-permute-start(f32[3,8,128]{2,1,0:T(8,128)S(1)} %get-tuple-element.23.own), channel_id=1, source_target_pairs={{0,16},{16,32},{32,48},{48,64},{64,80},{80,96},{96,112},{112,128},... | collective-permute-start | bytes 36872 | tf_op jit(solution)/shard_map/ppermute | solution.py:473
  23.0 14.8 %all-to-all-start = ((f32[16,8,512]{2,1,0:T(8,128)}), f32[16,8,512]{2,1,0:T(8,128)S(1)}, u32[]{:S(2)}, u32[]{:S(2)}) async-start(f32[16,8,512]{2,1,0:T(8,128)} %shard_map.39), calls=%async_computation | async-start | bytes 524288 | tf_op jit(solution)/shard_map/all_to_all | solution.py:486
  30.5 7.6 %collective-permute-start.3 = (f32[2,3,64,128]{3,2,1,0:T(8,128)S(1)}, f32[2,3,64,128]{3,2,1,0:T(8,128)S(1)}, u32[]{:S(2)}, u32[]{:S(2)}) collective-permute-start(f32[2,3,64,128]{3,2,1,0:T(8,128)S(1)} %get-tuple-element.29.own), channel_id=1, source_target_pairs={{16,0},{32,16},{48,32},{64,48},{80,64},{96,80},{112,96},{128,112},... | collective-permute-start | bytes 589832 | tf_op jit(solution)/shard_map/ppermute | solution.py:476
  30.5 7.6 %collective-permute-start.2 = (f32[2,3,64,128]{3,2,1,0:T(8,128)S(1)}, f32[2,3,64,128]{3,2,1,0:T(8,128)S(1)}, u32[]{:S(2)}, u32[]{:S(2)}) collective-permute-start(f32[2,3,64,128]{3,2,1,0:T(8,128)S(1)} %get-tuple-element.29.own), channel_id=1, source_target_pairs={{0,16},{16,32},{32,48},{48,64},{64,80},{80,96},{96,112},{112,128},... | collective-permute-start | bytes 589832 | tf_op jit(solution)/shard_map/ppermute | solution.py:474
  38.9 1.4 %collective-permute-start.5 = (f32[3,8,128]{2,1,0:T(8,128)S(1)}, f32[3,8,128]{2,1,0:T(8,128)S(1)}, u32[]{:S(2)}, u32[]{:S(2)}) collective-permute-start(f32[3,8,128]{2,1,0:T(8,128)S(1)} %get-tuple-element.32.own), channel_id=1, source_target_pairs={{16,0},{32,16},{48,32},{64,48},{80,64},{96,80},{112,96},{128,112},... | collective-permute-start | bytes 36872 | tf_op jit(solution)/shard_map/ppermute | solution.py:475
  38.9 4.3 %collective-permute-start.4 = (f32[3,8,128]{2,1,0:T(8,128)S(1)}, f32[3,8,128]{2,1,0:T(8,128)S(1)}, u32[]{:S(2)}, u32[]{:S(2)}) collective-permute-start(f32[3,8,128]{2,1,0:T(8,128)S(1)} %get-tuple-element.32.own), channel_id=1, source_target_pairs={{0,16},{16,32},{32,48},{48,64},{64,80},{80,96},{96,112},{112,128},... | collective-permute-start | bytes 36872 | tf_op jit(solution)/shard_map/ppermute | solution.py:473
  44.2 13.3 %all-to-all-start.1 = ((f32[16,8,512]{2,1,0:T(8,128)}), f32[16,8,512]{2,1,0:T(8,128)S(1)}, u32[]{:S(2)}, u32[]{:S(2)}) async-start(f32[16,8,512]{2,1,0:T(8,128)} %shard_map.43), calls=%async_computation.1 | async-start | bytes 524288 | tf_op jit(solution)/shard_map/all_to_all | solution.py:486
  50.2 7.6 %collective-permute-start.7 = (f32[2,3,64,128]{3,2,1,0:T(8,128)S(1)}, f32[2,3,64,128]{3,2,1,0:T(8,128)S(1)}, u32[]{:S(2)}, u32[]{:S(2)}) collective-permute-start(f32[2,3,64,128]{3,2,1,0:T(8,128)S(1)} %get-tuple-element.34.own), channel_id=1, source_target_pairs={{16,0},{32,16},{48,32},{64,48},{80,64},{96,80},{112,96},{128,112},... | collective-permute-start | bytes 589832 | tf_op jit(solution)/shard_map/ppermute | solution.py:476
  50.2 7.6 %collective-permute-start.6 = (f32[2,3,64,128]{3,2,1,0:T(8,128)S(1)}, f32[2,3,64,128]{3,2,1,0:T(8,128)S(1)}, u32[]{:S(2)}, u32[]{:S(2)}) collective-permute-start(f32[2,3,64,128]{3,2,1,0:T(8,128)S(1)} %get-tuple-element.34.own), channel_id=1, source_target_pairs={{0,16},{16,32},{32,48},{48,64},{64,80},{80,96},{96,112},{112,128},... | collective-permute-start | bytes 589832 | tf_op jit(solution)/shard_map/ppermute | solution.py:474

commit v6 on v5

--- a/solution.py
+++ b/solution.py
@@ -87,12 +87,17 @@
     return total
 
 
-def flux_moments(layer, flux):
-    kx = dt * jnp.abs(own_cx())
-    cy, cz = lane_velocities()
-    ky, kz = dt * jnp.abs(cy), dt * jnp.abs(cz)
+def flux_tables():
+    speeds = [dt * jnp.abs(c) for c in (own_cx(), *lane_velocities())]
+    _, cz = lane_velocities()
     table = moment_table()
     rising = jnp.broadcast_to(cz > 0, table.shape)
+    both = [jnp.where(rising, table, 0.0), jnp.where(rising, 0.0, table)]
+    return speeds, jnp.concatenate(both, axis=0).astype(jnp.bfloat16)
+
+
+def flux_moments(layer, flux, tables):
+    (kx, ky, kz), both = tables
     ups, downs = [], []
     for half in range(2):
         lanes = slice(half * HALF, (half + 1) * HALF)
@@ -100,14 +105,7 @@
             [layer(half, 0) * kx, layer(half, 1) * ky[:, lanes], layer(half, 2) * kz[:, lanes]],
             axis=0,
         )
-        both = jnp.concatenate(
-            [
-                jnp.where(rising[:, lanes], table[:, lanes], 0.0),
-                jnp.where(rising[:, lanes], 0.0, table[:, lanes]),
-            ],
-            axis=0,
-        )
-        term = times_transposed(both.astype(jnp.bfloat16), rows)
+        term = times_transposed(both[:, lanes], rows)
         ups.append(term[0:BS] + term[BS : 2 * BS])
         downs.append(term[2 * BS : 3 * BS] + term[3 * BS :])
     sums = [up + down for up, down in zip(ups, downs)]
@@ -120,16 +118,16 @@
     flux[2, :, GROUPS:] = (downs[0] + downs[1])[:, 2 * GROUPS :]
 
 
-def face_flux(faces, flux):
-    flux_moments(lambda half, dim: faces[half, dim], flux)
+def face_flux(faces, flux, tables):
+    flux_moments(lambda half, dim: faces[half, dim], flux, tables)
 
 
 def fill_kernel(
     dist_hbm, solid_hbm, table_hbm, filled, faces, flux, solid, neighbours, dist, sems
 ):
     copies = [
-        pltpu.make_async_copy(solid_hbm, solid, sems.at[0]),
-        pltpu.make_async_copy(dist_hbm, dist, sems.at[1]),
+        pltpu.make_async_copy(dist_hbm, dist, sems.at[0]),
+        pltpu.make_async_copy(solid_hbm, solid, sems.at[1]),
         pltpu.make_async_copy(table_hbm, neighbours, sems.at[2]),
     ]
     for copy in copies:
@@ -138,38 +136,25 @@
     cy, cz = lane_velocities()
     wall = maxwellian(20.0, 0.0, 2.0, cx, cy, cz)
     top = lax.broadcasted_iota(jnp.int32, (BS, HALF), 0) == 0
-    copies[0].wait()
+    tables = flux_tables()
+    copies[1].wait()
     flags = jnp.broadcast_to(solid[...].astype(F32), (BS, CELLS))
     mask = lax.dot_general(
         flags, top.astype(F32), (((0,), (0,)), ((), ())), preferred_element_type=F32
     )
     inside = mask > 0.5
-    copies[1].wait()
+    copies[0].wait()
     for half in range(2):
         lanes = slice(half * HALF, (half + 1) * HALF)
         filled[half] = jnp.where(inside, wall[:, lanes], dist[:, lanes])
     store_faces(filled, faces)
-    face_flux(faces, flux)
+    face_flux(faces, flux, tables)
     copies[2].wait()
 
 
 def upwind_edge(cz, sub):
     upward = jnp.broadcast_to(cz > 0, (BS, HALF))
     return upward, (sub == 0) & upward | (sub == BS - 1) & jnp.logical_not(upward)
-
-
-def spread_table():
-    row = lax.broadcasted_iota(jnp.int32, (2 * GROUPS, CELLS), 0)
-    cell = lax.broadcasted_iota(jnp.int32, (2 * GROUPS, CELLS), 1)
-    place = row & (GROUPS - 1)
-    later = row >= GROUPS
-    positive = lax.axis_index("vel") >= NVX // 2
-    first = jnp.where(positive, 0, (BS - 1) * GROUPS)
-    along_x = jnp.where(later, -1, first + place)
-    along_y = (place >> 3) * GROUPS + (place & (BS - 1)) + jnp.where(later, 0, GROUPS - BS)
-    along_z = place * BS + jnp.where(later, BS - 1, 0)
-    hits = [(cell == target).astype(F32) for target in (along_x, along_y, along_z)]
-    return jnp.concatenate(hits, axis=0).astype(jnp.bfloat16)
 
 
 def cell_basis():
@@ -191,13 +176,14 @@
     return jnp.concatenate([block] * 3, axis=0).astype(jnp.bfloat16)
 
 
-def first_inner_kernel(filled, inner, local, basis, spread, open_flux):
+def first_inner_kernel(filled, inner, local, basis, open_flux):
     basis[...] = cell_basis()
-    spread[...] = spread_table()
     cy, cz = lane_velocities()
     inflow = maxwellian(20.0, 2.5, 1.0, own_cx(), cy, cz)
     wide = jnp.broadcast_to(inflow, (GROUPS, LANES))
-    flux_moments(lambda half, dim: wide[:, half * HALF : (half + 1) * HALF], open_flux)
+    flux_moments(
+        lambda half, dim: wide[:, half * HALF : (half + 1) * HALF], open_flux, flux_tables()
+    )
     inner_kernel(filled, inner, local)
 
 
@@ -255,23 +241,37 @@
     return jnp.where(place == 3, opened, value)
 
 
-def join_kernel(neighbours, local, own, below, above, opened, spread, partial):
+def join_kernel(neighbours, local, own, below, above, opened, partial):
     face, face_x = source_places(neighbours)
-    early = lax.broadcasted_iota(jnp.int32, (BS, 2 * GROUPS), 1) < GROUPS
+    positive = lax.axis_index("vel") >= NVX // 2
+    lane = lax.broadcasted_iota(jnp.int32, (BS, 2 * GROUPS), 1)
+    early = lane < GROUPS
     places = [
         jnp.broadcast_to(face_x, early.shape),
         jnp.where(early, face[3], face[2]),
         jnp.where(early, face[4], face[5]),
     ]
-    columns = []
-    for dim, place in enumerate(places):
-        value = choose(place, below[dim], own[dim], above[dim], opened[dim])
-        pieces = bfloat_pieces(value)
-        columns.append(jnp.concatenate(pieces + [jnp.zeros_like(value)], axis=0))
-    left = jnp.concatenate(columns, axis=1).astype(jnp.bfloat16)
-    added = jnp.dot(left, spread[...], preferred_element_type=F32)
-    total = local[...] + (added[:BS] + added[BS : 2 * BS] + added[2 * BS : 3 * BS])
-    partial[...] = jnp.broadcast_to(total, (NVX, BS, CELLS))
+    along_x, along_y, along_z = [
+        choose(place, below[dim], own[dim], above[dim], opened[dim])
+        for dim, place in enumerate(places)
+    ]
+
+    def spread(value, source, where):
+        moved = jnp.take_along_axis(value, source, axis=1, mode="promise_in_bounds")
+        return jnp.where(where, moved, 0.0)
+
+    j, l = (lane >> 3) & (BS - 1), lane & (BS - 1)
+    for pair in range(BS // 2):
+        i = 2 * pair + (lane >> 6)
+        at_x = i == jnp.where(positive, 0, BS - 1)
+        total = spread(along_x, lane & (GROUPS - 1), at_x)
+        low, high = j == 0, j == BS - 1
+        total = total + spread(along_y, i * BS + l + jnp.where(low, GROUPS, 0), low | high)
+        low, high = l == 0, l == BS - 1
+        total = total + spread(along_z, i * BS + j + jnp.where(high, GROUPS, 0), low | high)
+        cells = slice(pair * 2 * GROUPS, (pair + 1) * 2 * GROUPS)
+        total = total + local[:, cells]
+        partial[:, :, cells] = jnp.broadcast_to(total, (NVX, BS, 2 * GROUPS))
 
 
 def add_ghosts(neighbours, inner, own, below, above, advected, ghost_z):
@@ -402,7 +402,7 @@
     add_ghosts(neighbours, inner, own, below, above, advected, ghost_z)
     collide(turned, basis, advected, [PIECE] * PIECES, store)
     store_faces(filled, faces)
-    face_flux(faces, flux)
+    face_flux(faces, flux, flux_tables())
 
 
 def last_kernel(
@@ -429,7 +429,6 @@
 FIELD = jax.ShapeDtypeStruct((2, CELLS, HALF), F32)
 RESULT = jax.ShapeDtypeStruct((CELLS, LANES), F32)
 FACES = jax.ShapeDtypeStruct((2, 3, GROUPS, HALF), F32)
-SPREAD = jax.ShapeDtypeStruct((6 * GROUPS, CELLS), jnp.bfloat16)
 FLUX = jax.ShapeDtypeStruct((3, BS, 2 * GROUPS), F32)
 LOCAL = jax.ShapeDtypeStruct((BS, CELLS), F32)
 SOLID = jax.ShapeDtypeStruct((1, CELLS), jnp.int32)
@@ -475,13 +474,13 @@
         flux_above = lax.ppermute(flux, "space", backward)
         above = lax.ppermute(faces, "space", backward)
         if step == 0:
-            inner, local, basis, spread, open_flux = call(
-                first_inner_kernel, [VMEM], [FIELD, LOCAL, BASIS, SPREAD, FLUX]
+            inner, local, basis, open_flux = call(
+                first_inner_kernel, [VMEM], [FIELD, LOCAL, BASIS, FLUX]
             )(filled)
         else:
             inner, local = call(inner_kernel, [VMEM], [FIELD, LOCAL])(filled)
-        (partial,) = call(join_kernel, [VMEM] * 7, [PARTIAL])(
-            neighbours, local, flux, flux_below, flux_above, open_flux, spread
+        (partial,) = call(join_kernel, [VMEM] * 6, [PARTIAL])(
+            neighbours, local, flux, flux_below, flux_above, open_flux
         )
         gathered = lax.all_to_all(partial, "vel", 0, 0, tiled=True)
         (turned,) = call(coefficient_kernel, [VMEM] * 2, [TURNED])(gathered, solid)

time: 59.3 us -> 59.2 us (level)
  no operation moved by 1% of the time
where the time goes in v6:
time: 59.2 us; the launch traced here: 58.8 us
  starting transfers between devices  31.2 us (53%)
  waiting for transfers between devices  21 us (35%)
  Pallas kernels  6.59 us (11%)
    ppermute x2, starting transfers between devices, on_device(): flux_above = lax.ppermute(flux, 'space', backward)  16.2 us
    all_to_all x2, waiting for transfers between devices, on_device(): gathered = lax.all_to_all(partial, 'vel', 0, 0, tiled=True)  13.6 us
    all_to_all x2, starting transfers between devices, on_device(): gathered = lax.all_to_all(partial, 'vel', 0, 0, tiled=True)  13.4 us
    ppermute x2, waiting for transfers between devices, on_device(): flux_below = lax.ppermute(flux, 'space', forward)  5.85 us
    pallas_call x2, Pallas kernels, on_device(): call(join_kernel, [VMEM] * 6, [PARTIAL])  1.92 us
    pallas_call x1, Pallas kernels, on_device(): call(fill_kernel, [HBM] * 3, [FIELD, FACES, FLUX, SOLID, TABLE], [pltpu.V...  1.49 us
    ppermute x2, waiting for transfers between devices, on_device(): flux_above = lax.ppermute(flux, 'space', backward)  1.46 us
  transfers between devices with their start and end apart: 10, of which 6 were waited for; matrix products, arithmetic and copies ran while one was open for 0% of the time, Pallas kernels for 2%

profile of v6, /device:TPU:2, one launch (start us, length us, event | category | flops | bytes accessed | tf_op | source)
XLA Modules:
  0.0 58.8 jit_solution(9331685282342782712)
XLA Ops:
  0.0 1.5 %shard_map.37 = (f32[2,512,128]{2,1,0:T(8,128)S(1)}, f32[2,3,64,128]{3,2,1,0:T(8,128)S(1)}, f32[3,8,128]{2,1,0:T(8,128)S(1)}, s32[1,512]{1,0:T(1,128)S(1)}, s32[1,6]{1,0:T(1,128)S(1)}) custom-call(f32[512,256]{1,0:T(8,128)} %bitcast.2, s32[1,512]{1,0:T(1,128)} %solid_hbm.1, s32[1,6]{1,0:T(1,128)} %table_hbm.1), custom_call_target="tpu_custom_call" | custom-call | flops 5242880 | bytes 1048576 | tf_op jit(solution)/shard_map/pallas_call | solution.py:461
  1.5 16.2 %collective-permute-start.1 = (f32[3,8,128]{2,1,0:T(8,128)S(1)}, f32[3,8,128]{2,1,0:T(8,128)S(1)}, u32[]{:S(2)}, u32[]{:S(2)}) collective-permute-start(f32[3,8,128]{2,1,0:T(8,128)S(1)} %get-tuple-element.22.own), channel_id=1, source_target_pairs={{16,0},{32,16},{48,32},{64,48},{80,64},{96,80},{112,96},{128,112},... | collective-permute-start | bytes 36872 | tf_op jit(solution)/shard_map/ppermute | solution.py:474
  17.7 0.0 collective-permute-start
  17.7 0.5 shard_map.38
  18.2 0.9 %collective-permute-done.1.above = f32[3,8,128]{2,1,0:T(8,128)S(1)} collective-permute-done((f32[3,8,128]{2,1,0:T(8,128)S(1)}, f32[3,8,128]{2,1,0:T(8,128)S(1)}, u32[]{:S(2)}, u32[]{:S(2)}) %collective-permute-start.1) | collective-permute-done | bytes 12320 | tf_op jit(solution)/shard_map/ppermute | solution.py:474
  19.1 2.9 %collective-permute-done.below = f32[3,8,128]{2,1,0:T(8,128)S(1)} collective-permute-done((f32[3,8,128]{2,1,0:T(8,128)S(1)}, f32[3,8,128]{2,1,0:T(8,128)S(1)}, u32[]{:S(2)}, u32[]{:S(2)}) %collective-permute-start) | collective-permute-done | bytes 12320 | tf_op jit(solution)/shard_map/ppermute | solution.py:472
  22.1 1.0 %shard_map.39 = f32[16,8,512]{2,1,0:T(8,128)} custom-call(s32[1,6]{1,0:T(1,128)S(1)} %get-tuple-element.19.neighbours, f32[8,512]{1,0:T(8,128)S(1)} %get-tuple-element.21.local, f32[3,8,128]{2,1,0:T(8,128)S(1)} %get-tuple-element.22.own, f32[3,8,128]{2,1,0:T(8,128)S(1)} %collective-permute-done.below, f32[3,8,128]{2,1,0:T(8,128)S(1)} %collective-permute-done.1.above, ...), custom_call_target="tpu_custom_call" | custom-call | flops 5242880 | bytes 1048576 | tf_op jit(solution)/shard_map/pallas_call | solution.py:482
  23.0 7.5 %all-to-all-start = ((f32[16,8,512]{2,1,0:T(8,128)}), f32[16,8,512]{2,1,0:T(8,128)S(1)}, u32[]{:S(2)}, u32[]{:S(2)}) async-start(f32[16,8,512]{2,1,0:T(8,128)} %shard_map.39), calls=%async_computation | async-start | bytes 524288 | tf_op jit(solution)/shard_map/all_to_all | solution.py:485
  30.5 0.0 collective-permute-start.3
  30.5 0.5 collective-permute-start.2
  31.0 6.8 %all-to-all-done.gathered = f32[16,8,512]{2,1,0:T(8,128)S(1)} async-done(((f32[16,8,512]{2,1,0:T(8,128)}), f32[16,8,512]{2,1,0:T(8,128)S(1)}, u32[]{:S(2)}, u32[]{:S(2)}) %all-to-all-start) | async-done | bytes 262176 | tf_op jit(solution)/shard_map/all_to_all | solution.py:485
  37.8 0.2 shard_map.40.turned
  38.1 0.0 collective-permute-done.2.below
  38.1 0.7 %shard_map.41 = (f32[2,512,128]{2,1,0:T(8,128)S(1)}, f32[2,3,64,128]{3,2,1,0:T(8,128)S(1)}, f32[3,8,128]{2,1,0:T(8,128)S(1)}) custom-call(bf16[512,48]{1,0:T(8,128)(2,1)S(1)} %shard_map.40.turned, bf16[48,768]{1,0:T(8,128)(2,1)S(1)} %get-tuple-element.25.basis, s32[1,6]{1,0:T(1,128)S(1)} %get-tuple-element.19.neighbours, ...), custom_call_target="tpu_custom_call" | custom-call | flops 5242880 | bytes 1048576 | tf_op jit(solution)/shard_map/pallas_call | solution.py:490
  38.8 0.5 collective-permute-start.4
  39.3 0.4 shard_map.42
  39.7 0.5 collective-permute-done.5.above
  40.2 2.9 %collective-permute-done.4.below = f32[3,8,128]{2,1,0:T(8,128)S(1)} collective-permute-done((f32[3,8,128]{2,1,0:T(8,128)S(1)}, f32[3,8,128]{2,1,0:T(8,128)S(1)}, u32[]{:S(2)}, u32[]{:S(2)}) %collective-permute-start.4) | collective-permute-done | bytes 12320 | tf_op jit(solution)/shard_map/ppermute | solution.py:472
  43.2 1.0 %shard_map.43 = f32[16,8,512]{2,1,0:T(8,128)} custom-call(s32[1,6]{1,0:T(1,128)S(1)} %get-tuple-element.19.neighbours, f32[8,512]{1,0:T(8,128)S(1)} %get-tuple-element.29.local, f32[3,8,128]{2,1,0:T(8,128)S(1)} %get-tuple-element.30.own, f32[3,8,128]{2,1,0:T(8,128)S(1)} %collective-permute-done.4.below, f32[3,8,128]{2,1,0:T(8,128)S(1)} %collective-permute-done.5.above, ...), custom_call_target="tpu_custom_call" | custom-call | flops 5242880 | bytes 1048576 | tf_op jit(solution)/shard_map/pallas_call | solution.py:482
  44.1 6.0 %all-to-all-start.1 = ((f32[16,8,512]{2,1,0:T(8,128)}), f32[16,8,512]{2,1,0:T(8,128)S(1)}, u32[]{:S(2)}, u32[]{:S(2)}) async-start(f32[16,8,512]{2,1,0:T(8,128)} %shard_map.43), calls=%async_computation.1 | async-start | bytes 524288 | tf_op jit(solution)/shard_map/all_to_all | solution.py:485
  50.1 0.5 collective-permute-start.6
  50.6 6.8 %all-to-all-done.1.gathered = f32[16,8,512]{2,1,0:T(8,128)S(1)} async-done(((f32[16,8,512]{2,1,0:T(8,128)}), f32[16,8,512]{2,1,0:T(8,128)S(1)}, u32[]{:S(2)}, u32[]{:S(2)}) %all-to-all-start.1) | async-done | bytes 262176 | tf_op jit(solution)/shard_map/all_to_all | solution.py:485
  57.4 0.2 shard_map.44.turned
  57.7 1.1 %shard_map.45 = f32[512,256]{1,0:T(8,128)} custom-call(bf16[512,48]{1,0:T(8,128)(2,1)S(1)} %shard_map.44.turned, bf16[48,768]{1,0:T(8,128)(2,1)S(1)} %get-tuple-element.25.basis, s32[1,6]{1,0:T(1,128)S(1)} %get-tuple-element.19.neighbours, f32[2,512,128]{2,1,0:T(8,128)S(1)} %get-tuple-element.31.inner, f32[2,3,64,128]{3,2,1,0:T(8,128)S(1)} %get-tuple-element.32.own, ...), custom_call_target="tpu_custom_call" | custom-call | flops 5242880 | bytes 1048576 | tf_op jit(solution)/shard_map/pallas_call | solution.py:495
  (5 shorter events, 0.0 us)
Async XLA Ops:
  1.5 17.6 %collective-permute-start.1 = (f32[3,8,128]{2,1,0:T(8,128)S(1)}, f32[3,8,128]{2,1,0:T(8,128)S(1)}, u32[]{:S(2)}, u32[]{:S(2)}) collective-permute-start(f32[3,8,128]{2,1,0:T(8,128)S(1)} %get-tuple-element.22.own), channel_id=1, source_target_pairs={{16,0},{32,16},{48,32},{64,48},{80,64},{96,80},{112,96},{128,112},... | collective-permute-start | bytes 36872 | tf_op jit(solution)/shard_map/ppermute | solution.py:474
  17.7 4.3 %collective-permute-start = (f32[3,8,128]{2,1,0:T(8,128)S(1)}, f32[3,8,128]{2,1,0:T(8,128)S(1)}, u32[]{:S(2)}, u32[]{:S(2)}) collective-permute-start(f32[3,8,128]{2,1,0:T(8,128)S(1)} %get-tuple-element.22.own), channel_id=1, source_target_pairs={{0,16},{16,32},{32,48},{48,64},{64,80},{80,96},{96,112},{112,128},... | collective-permute-start | bytes 36872 | tf_op jit(solution)/shard_map/ppermute | solution.py:472
  23.0 14.8 %all-to-all-start = ((f32[16,8,512]{2,1,0:T(8,128)}), f32[16,8,512]{2,1,0:T(8,128)S(1)}, u32[]{:S(2)}, u32[]{:S(2)}) async-start(f32[16,8,512]{2,1,0:T(8,128)} %shard_map.39), calls=%async_computation | async-start | bytes 524288 | tf_op jit(solution)/shard_map/all_to_all | solution.py:485
  30.5 7.6 %collective-permute-start.3 = (f32[2,3,64,128]{3,2,1,0:T(8,128)S(1)}, f32[2,3,64,128]{3,2,1,0:T(8,128)S(1)}, u32[]{:S(2)}, u32[]{:S(2)}) collective-permute-start(f32[2,3,64,128]{3,2,1,0:T(8,128)S(1)} %get-tuple-element.27.own), channel_id=1, source_target_pairs={{16,0},{32,16},{48,32},{64,48},{80,64},{96,80},{112,96},{128,112},... | collective-permute-start | bytes 589832 | tf_op jit(solution)/shard_map/ppermute | solution.py:475
  30.5 7.6 %collective-permute-start.2 = (f32[2,3,64,128]{3,2,1,0:T(8,128)S(1)}, f32[2,3,64,128]{3,2,1,0:T(8,128)S(1)}, u32[]{:S(2)}, u32[]{:S(2)}) collective-permute-start(f32[2,3,64,128]{3,2,1,0:T(8,128)S(1)} %get-tuple-element.27.own), channel_id=1, source_target_pairs={{0,16},{16,32},{32,48},{48,64},{64,80},{80,96},{96,112},{112,128},... | collective-permute-start | bytes 589832 | tf_op jit(solution)/shard_map/ppermute | solution.py:473
  38.8 1.4 %collective-permute-start.5 = (f32[3,8,128]{2,1,0:T(8,128)S(1)}, f32[3,8,128]{2,1,0:T(8,128)S(1)}, u32[]{:S(2)}, u32[]{:S(2)}) collective-permute-start(f32[3,8,128]{2,1,0:T(8,128)S(1)} %get-tuple-element.30.own), channel_id=1, source_target_pairs={{16,0},{32,16},{48,32},{64,48},{80,64},{96,80},{112,96},{128,112},... | collective-permute-start | bytes 36872 | tf_op jit(solution)/shard_map/ppermute | solution.py:474
  38.8 4.3 %collective-permute-start.4 = (f32[3,8,128]{2,1,0:T(8,128)S(1)}, f32[3,8,128]{2,1,0:T(8,128)S(1)}, u32[]{:S(2)}, u32[]{:S(2)}) collective-permute-start(f32[3,8,128]{2,1,0:T(8,128)S(1)} %get-tuple-element.30.own), channel_id=1, source_target_pairs={{0,16},{16,32},{32,48},{48,64},{64,80},{80,96},{96,112},{112,128},... | collective-permute-start | bytes 36872 | tf_op jit(solution)/shard_map/ppermute | solution.py:472
  44.1 13.3 %all-to-all-start.1 = ((f32[16,8,512]{2,1,0:T(8,128)}), f32[16,8,512]{2,1,0:T(8,128)S(1)}, u32[]{:S(2)}, u32[]{:S(2)}) async-start(f32[16,8,512]{2,1,0:T(8,128)} %shard_map.43), calls=%async_computation.1 | async-start | bytes 524288 | tf_op jit(solution)/shard_map/all_to_all | solution.py:485
  50.1 7.6 %collective-permute-start.7 = (f32[2,3,64,128]{3,2,1,0:T(8,128)S(1)}, f32[2,3,64,128]{3,2,1,0:T(8,128)S(1)}, u32[]{:S(2)}, u32[]{:S(2)}) collective-permute-start(f32[2,3,64,128]{3,2,1,0:T(8,128)S(1)} %get-tuple-element.32.own), channel_id=1, source_target_pairs={{16,0},{32,16},{48,32},{64,48},{80,64},{96,80},{112,96},{128,112},... | collective-permute-start | bytes 589832 | tf_op jit(solution)/shard_map/ppermute | solution.py:475
  50.1 7.6 %collective-permute-start.6 = (f32[2,3,64,128]{3,2,1,0:T(8,128)S(1)}, f32[2,3,64,128]{3,2,1,0:T(8,128)S(1)}, u32[]{:S(2)}, u32[]{:S(2)}) collective-permute-start(f32[2,3,64,128]{3,2,1,0:T(8,128)S(1)} %get-tuple-element.32.own), channel_id=1, source_target_pairs={{0,16},{16,32},{32,48},{48,64},{64,80},{80,96},{96,112},{112,128},... | collective-permute-start | bytes 589832 | tf_op jit(solution)/shard_map/ppermute | solution.py:473

commit v7 on v6

--- a/solution.py
+++ b/solution.py
@@ -57,10 +57,6 @@
         top = filled[half, pl.ds(BS - 1, GROUPS, stride=BS), :]
         upward = cz[:, half * HALF : (half + 1) * HALF] > 0
         faces[half, 2] = jnp.where(upward, top, bottom)
-
-
-PIECES = 4
-PIECE = CELLS // PIECES
 
 
 def two_pieces(value):
@@ -126,8 +122,8 @@
     dist_hbm, solid_hbm, table_hbm, filled, faces, flux, solid, neighbours, dist, sems
 ):
     copies = [
-        pltpu.make_async_copy(dist_hbm, dist, sems.at[0]),
-        pltpu.make_async_copy(solid_hbm, solid, sems.at[1]),
+        pltpu.make_async_copy(solid_hbm, solid, sems.at[0]),
+        pltpu.make_async_copy(dist_hbm, dist, sems.at[1]),
         pltpu.make_async_copy(table_hbm, neighbours, sems.at[2]),
     ]
     for copy in copies:
@@ -137,13 +133,13 @@
     wall = maxwellian(20.0, 0.0, 2.0, cx, cy, cz)
     top = lax.broadcasted_iota(jnp.int32, (BS, HALF), 0) == 0
     tables = flux_tables()
-    copies[1].wait()
+    copies[0].wait()
     flags = jnp.broadcast_to(solid[...].astype(F32), (BS, CELLS))
     mask = lax.dot_general(
         flags, top.astype(F32), (((0,), (0,)), ((), ())), preferred_element_type=F32
     )
     inside = mask > 0.5
-    copies[0].wait()
+    copies[1].wait()
     for half in range(2):
         lanes = slice(half * HALF, (half + 1) * HALF)
         filled[half] = jnp.where(inside, wall[:, lanes], dist[:, lanes])
@@ -400,7 +396,7 @@
         filled[half, first : first + count] = value
 
     add_ghosts(neighbours, inner, own, below, above, advected, ghost_z)
-    collide(turned, basis, advected, [PIECE] * PIECES, store)
+    collide(turned, basis, advected, [GROUPS] * BS, store)
     store_faces(filled, faces)
     face_flux(faces, flux, flux_tables())
 

time: 59.2 us -> 59.2 us (level)
  no operation moved by 1% of the time
where the time goes in v7:
time: 59.2 us; the launch traced here: 58.8 us
  starting transfers between devices  31.2 us (53%)
  waiting for transfers between devices  21 us (35%)
  Pallas kernels  6.53 us (11%)
    ppermute x2, starting transfers between devices, on_device(): flux_above = lax.ppermute(flux, 'space', backward)  16.2 us
    all_to_all x2, waiting for transfers between devices, on_device(): gathered = lax.all_to_all(partial, 'vel', 0, 0, tiled=True)  13.6 us
    all_to_all x2, starting transfers between devices, on_device(): gathered = lax.all_to_all(partial, 'vel', 0, 0, tiled=True)  13.4 us
    ppermute x2, waiting for transfers between devices, on_device(): flux_below = lax.ppermute(flux, 'space', forward)  5.85 us
    pallas_call x2, Pallas kernels, on_device(): call(join_kernel, [VMEM] * 6, [PARTIAL])  1.92 us
    ppermute x2, waiting for transfers between devices, on_device(): flux_above = lax.ppermute(flux, 'space', backward)  1.46 us
    pallas_call x1, Pallas kernels, on_device(): call(fill_kernel, [HBM] * 3, [FIELD, FACES, FLUX, SOLID, TABLE], [pltpu.V...  1.45 us
  transfers between devices with their start and end apart: 10, of which 6 were waited for; matrix products, arithmetic and copies ran while one was open for 0% of the time, Pallas kernels for 2%

profile of v7, /device:TPU:2, one launch (start us, length us, event | category | flops | bytes accessed | tf_op | source)
XLA Modules:
  0.0 58.8 jit_solution(17583605210303821845)
XLA Ops:
  0.0 1.4 %shard_map.37 = (f32[2,512,128]{2,1,0:T(8,128)S(1)}, f32[2,3,64,128]{3,2,1,0:T(8,128)S(1)}, f32[3,8,128]{2,1,0:T(8,128)S(1)}, s32[1,512]{1,0:T(1,128)S(1)}, s32[1,6]{1,0:T(1,128)S(1)}) custom-call(f32[512,256]{1,0:T(8,128)} %bitcast.2, s32[1,512]{1,0:T(1,128)} %solid_hbm.1, s32[1,6]{1,0:T(1,128)} %table_hbm.1), custom_call_target="tpu_custom_call" | custom-call | flops 5242880 | bytes 1048576 | tf_op jit(solution)/shard_map/pallas_call | solution.py:457
  1.5 16.2 %collective-permute-start.1 = (f32[3,8,128]{2,1,0:T(8,128)S(1)}, f32[3,8,128]{2,1,0:T(8,128)S(1)}, u32[]{:S(2)}, u32[]{:S(2)}) collective-permute-start(f32[3,8,128]{2,1,0:T(8,128)S(1)} %get-tuple-element.22.own), channel_id=1, source_target_pairs={{16,0},{32,16},{48,32},{64,48},{80,64},{96,80},{112,96},{128,112},... | collective-permute-start | bytes 36872 | tf_op jit(solution)/shard_map/ppermute | solution.py:470
  17.7 0.5 shard_map.38
  18.1 0.9 %collective-permute-done.1.above = f32[3,8,128]{2,1,0:T(8,128)S(1)} collective-permute-done((f32[3,8,128]{2,1,0:T(8,128)S(1)}, f32[3,8,128]{2,1,0:T(8,128)S(1)}, u32[]{:S(2)}, u32[]{:S(2)}) %collective-permute-start.1) | collective-permute-done | bytes 12320 | tf_op jit(solution)/shard_map/ppermute | solution.py:470
  19.1 2.9 %collective-permute-done.below = f32[3,8,128]{2,1,0:T(8,128)S(1)} collective-permute-done((f32[3,8,128]{2,1,0:T(8,128)S(1)}, f32[3,8,128]{2,1,0:T(8,128)S(1)}, u32[]{:S(2)}, u32[]{:S(2)}) %collective-permute-start) | collective-permute-done | bytes 12320 | tf_op jit(solution)/shard_map/ppermute | solution.py:468
  22.0 1.0 %shard_map.39 = f32[16,8,512]{2,1,0:T(8,128)} custom-call(s32[1,6]{1,0:T(1,128)S(1)} %get-tuple-element.19.neighbours, f32[8,512]{1,0:T(8,128)S(1)} %get-tuple-element.21.local, f32[3,8,128]{2,1,0:T(8,128)S(1)} %get-tuple-element.22.own, f32[3,8,128]{2,1,0:T(8,128)S(1)} %collective-permute-done.below, f32[3,8,128]{2,1,0:T(8,128)S(1)} %collective-permute-done.1.above, ...), custom_call_target="tpu_custom_call" | custom-call | flops 5242880 | bytes 1048576 | tf_op jit(solution)/shard_map/pallas_call | solution.py:478
  23.0 7.5 %all-to-all-start = ((f32[16,8,512]{2,1,0:T(8,128)}), f32[16,8,512]{2,1,0:T(8,128)S(1)}, u32[]{:S(2)}, u32[]{:S(2)}) async-start(f32[16,8,512]{2,1,0:T(8,128)} %shard_map.39), calls=%async_computation | async-start | bytes 524288 | tf_op jit(solution)/shard_map/all_to_all | solution.py:481
  30.5 0.5 collective-permute-start.2
  31.0 6.8 %all-to-all-done.gathered = f32[16,8,512]{2,1,0:T(8,128)S(1)} async-done(((f32[16,8,512]{2,1,0:T(8,128)}), f32[16,8,512]{2,1,0:T(8,128)S(1)}, u32[]{:S(2)}, u32[]{:S(2)}) %all-to-all-start) | async-done | bytes 262176 | tf_op jit(solution)/shard_map/all_to_all | solution.py:481
  37.8 0.2 shard_map.40.turned
  38.0 0.0 collective-permute-done.3.above
  38.0 0.0 collective-permute-done.2.below
  38.0 0.7 %shard_map.41 = (f32[2,512,128]{2,1,0:T(8,128)S(1)}, f32[2,3,64,128]{3,2,1,0:T(8,128)S(1)}, f32[3,8,128]{2,1,0:T(8,128)S(1)}) custom-call(bf16[512,48]{1,0:T(8,128)(2,1)S(1)} %shard_map.40.turned, bf16[48,768]{1,0:T(8,128)(2,1)S(1)} %get-tuple-element.25.basis, s32[1,6]{1,0:T(1,128)S(1)} %get-tuple-element.19.neighbours, ...), custom_call_target="tpu_custom_call" | custom-call | flops 5242880 | bytes 1048576 | tf_op jit(solution)/shard_map/pallas_call | solution.py:486
  38.8 0.0 collective-permute-start.5
  38.8 0.5 collective-permute-start.4
  39.3 0.4 shard_map.42
  39.7 0.5 collective-permute-done.5.above
  40.2 2.9 %collective-permute-done.4.below = f32[3,8,128]{2,1,0:T(8,128)S(1)} collective-permute-done((f32[3,8,128]{2,1,0:T(8,128)S(1)}, f32[3,8,128]{2,1,0:T(8,128)S(1)}, u32[]{:S(2)}, u32[]{:S(2)}) %collective-permute-start.4) | collective-permute-done | bytes 12320 | tf_op jit(solution)/shard_map/ppermute | solution.py:468
  43.1 1.0 %shard_map.43 = f32[16,8,512]{2,1,0:T(8,128)} custom-call(s32[1,6]{1,0:T(1,128)S(1)} %get-tuple-element.19.neighbours, f32[8,512]{1,0:T(8,128)S(1)} %get-tuple-element.29.local, f32[3,8,128]{2,1,0:T(8,128)S(1)} %get-tuple-element.30.own, f32[3,8,128]{2,1,0:T(8,128)S(1)} %collective-permute-done.4.below, f32[3,8,128]{2,1,0:T(8,128)S(1)} %collective-permute-done.5.above, ...), custom_call_target="tpu_custom_call" | custom-call | flops 5242880 | bytes 1048576 | tf_op jit(solution)/shard_map/pallas_call | solution.py:478
  44.1 6.0 %all-to-all-start.1 = ((f32[16,8,512]{2,1,0:T(8,128)}), f32[16,8,512]{2,1,0:T(8,128)S(1)}, u32[]{:S(2)}, u32[]{:S(2)}) async-start(f32[16,8,512]{2,1,0:T(8,128)} %shard_map.43), calls=%async_computation.1 | async-start | bytes 524288 | tf_op jit(solution)/shard_map/all_to_all | solution.py:481
  50.1 0.5 collective-permute-start.6
  50.6 6.8 %all-to-all-done.1.gathered = f32[16,8,512]{2,1,0:T(8,128)S(1)} async-done(((f32[16,8,512]{2,1,0:T(8,128)}), f32[16,8,512]{2,1,0:T(8,128)S(1)}, u32[]{:S(2)}, u32[]{:S(2)}) %all-to-all-start.1) | async-done | bytes 262176 | tf_op jit(solution)/shard_map/all_to_all | solution.py:481
  57.4 0.2 shard_map.44.turned
  57.6 1.1 %shard_map.45 = f32[512,256]{1,0:T(8,128)} custom-call(bf16[512,48]{1,0:T(8,128)(2,1)S(1)} %shard_map.44.turned, bf16[48,768]{1,0:T(8,128)(2,1)S(1)} %get-tuple-element.25.basis, s32[1,6]{1,0:T(1,128)S(1)} %get-tuple-element.19.neighbours, f32[2,512,128]{2,1,0:T(8,128)S(1)} %get-tuple-element.31.inner, f32[2,3,64,128]{3,2,1,0:T(8,128)S(1)} %get-tuple-element.32.own, ...), custom_call_target="tpu_custom_call" | custom-call | flops 5242880 | bytes 1048576 | tf_op jit(solution)/shard_map/pallas_call | solution.py:491
  (5 shorter events, 0.0 us)
Async XLA Ops:
  1.5 17.6 %collective-permute-start.1 = (f32[3,8,128]{2,1,0:T(8,128)S(1)}, f32[3,8,128]{2,1,0:T(8,128)S(1)}, u32[]{:S(2)}, u32[]{:S(2)}) collective-permute-start(f32[3,8,128]{2,1,0:T(8,128)S(1)} %get-tuple-element.22.own), channel_id=1, source_target_pairs={{16,0},{32,16},{48,32},{64,48},{80,64},{96,80},{112,96},{128,112},... | collective-permute-start | bytes 36872 | tf_op jit(solution)/shard_map/ppermute | solution.py:470
  17.7 4.3 %collective-permute-start = (f32[3,8,128]{2,1,0:T(8,128)S(1)}, f32[3,8,128]{2,1,0:T(8,128)S(1)}, u32[]{:S(2)}, u32[]{:S(2)}) collective-permute-start(f32[3,8,128]{2,1,0:T(8,128)S(1)} %get-tuple-element.22.own), channel_id=1, source_target_pairs={{0,16},{16,32},{32,48},{48,64},{64,80},{80,96},{96,112},{112,128},... | collective-permute-start | bytes 36872 | tf_op jit(solution)/shard_map/ppermute | solution.py:468
  23.0 14.8 %all-to-all-start = ((f32[16,8,512]{2,1,0:T(8,128)}), f32[16,8,512]{2,1,0:T(8,128)S(1)}, u32[]{:S(2)}, u32[]{:S(2)}) async-start(f32[16,8,512]{2,1,0:T(8,128)} %shard_map.39), calls=%async_computation | async-start | bytes 524288 | tf_op jit(solution)/shard_map/all_to_all | solution.py:481
  30.4 7.6 %collective-permute-start.3 = (f32[2,3,64,128]{3,2,1,0:T(8,128)S(1)}, f32[2,3,64,128]{3,2,1,0:T(8,128)S(1)}, u32[]{:S(2)}, u32[]{:S(2)}) collective-permute-start(f32[2,3,64,128]{3,2,1,0:T(8,128)S(1)} %get-tuple-element.27.own), channel_id=1, source_target_pairs={{16,0},{32,16},{48,32},{64,48},{80,64},{96,80},{112,96},{128,112},... | collective-permute-start | bytes 589832 | tf_op jit(solution)/shard_map/ppermute | solution.py:471
  30.5 7.6 %collective-permute-start.2 = (f32[2,3,64,128]{3,2,1,0:T(8,128)S(1)}, f32[2,3,64,128]{3,2,1,0:T(8,128)S(1)}, u32[]{:S(2)}, u32[]{:S(2)}) collective-permute-start(f32[2,3,64,128]{3,2,1,0:T(8,128)S(1)} %get-tuple-element.27.own), channel_id=1, source_target_pairs={{0,16},{16,32},{32,48},{48,64},{64,80},{80,96},{96,112},{112,128},... | collective-permute-start | bytes 589832 | tf_op jit(solution)/shard_map/ppermute | solution.py:469
  38.8 1.4 %collective-permute-start.5 = (f32[3,8,128]{2,1,0:T(8,128)S(1)}, f32[3,8,128]{2,1,0:T(8,128)S(1)}, u32[]{:S(2)}, u32[]{:S(2)}) collective-permute-start(f32[3,8,128]{2,1,0:T(8,128)S(1)} %get-tuple-element.30.own), channel_id=1, source_target_pairs={{16,0},{32,16},{48,32},{64,48},{80,64},{96,80},{112,96},{128,112},... | collective-permute-start | bytes 36872 | tf_op jit(solution)/shard_map/ppermute | solution.py:470
  38.8 4.3 %collective-permute-start.4 = (f32[3,8,128]{2,1,0:T(8,128)S(1)}, f32[3,8,128]{2,1,0:T(8,128)S(1)}, u32[]{:S(2)}, u32[]{:S(2)}) collective-permute-start(f32[3,8,128]{2,1,0:T(8,128)S(1)} %get-tuple-element.30.own), channel_id=1, source_target_pairs={{0,16},{16,32},{32,48},{48,64},{64,80},{80,96},{96,112},{112,128},... | collective-permute-start | bytes 36872 | tf_op jit(solution)/shard_map/ppermute | solution.py:468
  44.1 13.3 %all-to-all-start.1 = ((f32[16,8,512]{2,1,0:T(8,128)}), f32[16,8,512]{2,1,0:T(8,128)S(1)}, u32[]{:S(2)}, u32[]{:S(2)}) async-start(f32[16,8,512]{2,1,0:T(8,128)} %shard_map.43), calls=%async_computation.1 | async-start | bytes 524288 | tf_op jit(solution)/shard_map/all_to_all | solution.py:481
  50.1 7.6 %collective-permute-start.7 = (f32[2,3,64,128]{3,2,1,0:T(8,128)S(1)}, f32[2,3,64,128]{3,2,1,0:T(8,128)S(1)}, u32[]{:S(2)}, u32[]{:S(2)}) collective-permute-start(f32[2,3,64,128]{3,2,1,0:T(8,128)S(1)} %get-tuple-element.32.own), channel_id=1, source_target_pairs={{16,0},{32,16},{48,32},{64,48},{80,64},{96,80},{112,96},{128,112},... | collective-permute-start | bytes 589832 | tf_op jit(solution)/shard_map/ppermute | solution.py:471
  50.1 7.6 %collective-permute-start.6 = (f32[2,3,64,128]{3,2,1,0:T(8,128)S(1)}, f32[2,3,64,128]{3,2,1,0:T(8,128)S(1)}, u32[]{:S(2)}, u32[]{:S(2)}) collective-permute-start(f32[2,3,64,128]{3,2,1,0:T(8,128)S(1)} %get-tuple-element.32.own), channel_id=1, source_target_pairs={{0,16},{16,32},{32,48},{48,64},{64,80},{80,96},{96,112},{112,128},... | collective-permute-start | bytes 589832 | tf_op jit(solution)/shard_map/ppermute | solution.py:469
